TPU v7x, 32 devices: a whole 2x2x4 slice. The times are simulated.
32 devices in a mesh: grp: 4 (over y, x), seq: 8 (over z, core).
Axes of the slice: x: 2, y: 2, z: 4, core: 2. Of those that a mesh axis runs over, the one named last changes fastest.
Arguments:
- acoustic_sequence: bfloat16 [8192, 1536], P('seq'), may hold values from -6 to 6
- entry_rescale_factors: float32 [1536], replicated, may hold values from 0.1 to 1.9
- unitwise_entry_coefficients: bfloat16 [1536, 2, 1536], P(None, None, 'grp'), may hold values from -0.15625 to 0.15625
- channelwise_filter_taps: float32 [31, 1536], P(None, 'grp'), as said below
- filtering_rescale_factors: float32 [1536], P('grp'), may hold values from 0.1 to 1.9
- unitwise_exit_coefficients: bfloat16 [1536, 1536], P('grp'), may hold values from -0.15625 to 0.15625
- accumulation_coefficients: float32 [8192], P('seq'), may hold values from 0.03 to 0.3
- spike_indicator: int32 [8192], P('seq'), may hold values from 0 to 1, as said below
- textside_token_vectors: bfloat16 [1024, 4096], P('seq'), may hold values from -2 to 2
- textside_rescale_factors: float32 [4096], replicated, may hold values from 0.25 to 2.5
- probe_projection_coefficients: bfloat16 [4096, 2048], P(None, 'grp'), may hold values from -0.09375 to 0.09375
- probe_rescale_factors: float32 [128], replicated, may hold values from 0.5 to 1.5
- address_projection_coefficients: bfloat16 [1536, 512], P('grp'), may hold values from -0.15625 to 0.15625
- content_projection_coefficients: bfloat16 [1536, 512], P('grp'), may hold values from -0.15625 to 0.15625
- address_rescale_factors: float32 [128], replicated, may hold values from 0.25 to 2.5
- mixing_exit_coefficients: bfloat16 [2048, 4096], P('grp', 'seq'), may hold values from -0.125 to 0.125
Outputs:
- frames_out: bfloat16 [8192, 1536], P('seq', 'grp')
- pooled_out: bfloat16 [2048, 1536], P('seq', 'grp')
- dec_out: bfloat16 [1024, 4096], P('seq', 'grp')
Inputs may be any that keep to these rules, and one draw needn't show every extreme that they name: `spike_indicator`: 1 marks the last frame of a pooled row; the last frame fires; each block of 1024 frames holds 1 to 255 firings, 1024 in all. `channelwise_filter_taps`: depthwise taps.
All inputs are finite; a program needn't handle non-finite values.
Results may differ from a plain program's by a relative error of at most 0.014.
Values may be sent and summed in bfloat16 or wider, within the bound.
A program may use at most 128 MiB of HBM per device.

v0:
```python
import jax
import jax.numpy as jnp
from jax import lax
from jax.sharding import PartitionSpec as P

CAPL = 256


EPS_LAYER = 1e-05
EPS_ROOT = 1e-06
SCORE_SCALE = 0.25


def with_halo(cells, sides, width):
    for axis, dim in sides:
        count = lax.axis_size(axis)
        ends = count - 1
        head = lax.slice_in_dim(cells, 0, width, axis=dim)
        tail = lax.slice_in_dim(cells, cells.shape[dim] - width, cells.shape[dim], axis=dim)
        cells = jnp.concatenate(
            [
                lax.ppermute(tail, axis, [(i, (i + 1) % count) for i in range(ends)]),
                cells,
                lax.ppermute(head, axis, [((i + 1) % count, i) for i in range(ends)]),
            ],
            axis=dim,
        )
    return cells


def entering(value, axis, join, neutral):
    count, mine = (lax.axis_size(axis), lax.axis_index(axis))
    pieces = jax.tree.map(lambda part: lax.all_gather(part, axis), value)
    so_far = jax.tree.map(
        lambda part, zero: jnp.full_like(part, 0) + jnp.asarray(zero, part.dtype), value, neutral
    )

    def hop(position, so_far):
        longer = join(so_far, jax.tree.map(lambda part: part[position], pieces))
        return jax.tree.map(lambda new, old: jnp.where(position < mine, new, old), longer, so_far)

    return lax.fori_loop(0, count - 1, hop, so_far)


def layer_norm(inputs, scales):
    center = jnp.mean(inputs, axis=-1, keepdims=True)
    variance = jnp.mean((inputs - center) * (inputs - center), axis=-1, keepdims=True)
    return (inputs - center) * lax.rsqrt(variance + EPS_LAYER) * scales


def rms_scale(inputs, scales):
    return inputs * lax.rsqrt(jnp.mean(inputs * inputs, axis=-1, keepdims=True) + EPS_ROOT) * scales


def join_open(earlier, later_part):
    total = earlier[0] + later_part[0]
    open_sum = jnp.where(later_part[0] > 0, later_part[1], earlier[1] + later_part[1])
    return (total, open_sum)


def attend_block(packed_piece, live_piece, queries, head_dim):
    key_piece = packed_piece[..., :head_dim]
    value_piece = packed_piece[..., head_dim:]
    scores = (
        jnp.einsum("tgrd,ngd->tgrn", queries, key_piece, preferred_element_type=jnp.float32)
        * SCORE_SCALE
    )
    weights = jnp.exp(scores)
    weights = weights * live_piece.astype(jnp.float32)[None, None, None, :]
    numerator = jnp.einsum(
        "tgrn,ngd->tgrd",
        weights.astype(jnp.bfloat16),
        value_piece,
        preferred_element_type=jnp.float32,
    )
    return (numerator, jnp.sum(weights, axis=-1))


def local(
    acoustic_sequence,
    entry_rescale_factors,
    unitwise_entry_coefficients,
    channelwise_filter_taps,
    filtering_rescale_factors,
    unitwise_exit_coefficients,
    accumulation_coefficients,
    spike_indicator,
    textside_token_vectors,
    textside_rescale_factors,
    probe_projection_coefficients,
    probe_rescale_factors,
    address_projection_coefficients,
    content_projection_coefficients,
    address_rescale_factors,
    mixing_exit_coefficients,
):
    frame_count, feature_width = acoustic_sequence.shape
    columns = unitwise_entry_coefficients.shape[2]
    grp_index = lax.axis_index("grp")
    head_dim = probe_rescale_factors.shape[0]
    query_count = textside_token_vectors.shape[0]
    frames_f = acoustic_sequence.astype(jnp.float32)
    normed = layer_norm(frames_f, entry_rescale_factors).astype(jnp.bfloat16)
    projected = jnp.dot(
        normed,
        unitwise_entry_coefficients.reshape(feature_width, 2 * columns),
        preferred_element_type=jnp.float32,
    ).reshape(frame_count, 2, columns)
    gated = (projected[:, 0] * jax.nn.sigmoid(projected[:, 1])).astype(jnp.bfloat16)
    tap_total = channelwise_filter_taps.shape[0]
    rim_width = tap_total // 2
    widened = with_halo(gated, (("seq", 0),), rim_width)
    mixed_conv = jnp.zeros((frame_count, columns), jnp.float32)
    for tap_index in range(tap_total):
        mixed_conv = mixed_conv + channelwise_filter_taps[tap_index] * widened[
            tap_index : tap_index + frame_count
        ].astype(jnp.float32)
    totals, squares = lax.psum(
        (jnp.sum(mixed_conv, axis=1), jnp.sum(mixed_conv * mixed_conv, axis=1)), "grp"
    )
    center = totals / feature_width
    variance = squares / feature_width - center * center
    normal_part = (
        (mixed_conv - center[:, None])
        * lax.rsqrt(variance[:, None] + EPS_LAYER)
        * filtering_rescale_factors
    )
    activated = (normal_part * jax.nn.sigmoid(normal_part)).astype(jnp.bfloat16)
    branch = lax.psum_scatter(
        jnp.dot(activated, unitwise_exit_coefficients, preferred_element_type=jnp.float32),
        "grp",
        scatter_dimension=1,
        tiled=True,
    )
    residual_part = lax.dynamic_slice_in_dim(frames_f, grp_index * columns, columns, 1)
    hidden = residual_part + branch
    frames_out = hidden.astype(jnp.bfloat16)
    prior_coefficient = jnp.cumsum(spike_indicator) - spike_indicator
    accumulated_amount = jnp.sum(spike_indicator)
    weighted = accumulation_coefficients[:, None] * hidden
    in_tail = (prior_coefficient == accumulated_amount).astype(jnp.float32)
    tail_sum = jnp.sum(weighted * in_tail[:, None], axis=0)
    identity = (jnp.zeros((), jnp.float32), jnp.zeros((columns,), jnp.float32))
    prefix_count, carried = entering(
        (accumulated_amount.astype(jnp.float32), tail_sum), "seq", join_open, identity
    )
    slot_ids = jnp.arange(CAPL, dtype=jnp.int32)
    selector = (
        (slot_ids[:, None] == prior_coefficient[None, :])
        & (prior_coefficient[None, :] < accumulated_amount)
    ).astype(jnp.float32)
    pooled_f = jnp.dot(selector, weighted, precision=lax.Precision.HIGHEST)
    pooled_f = pooled_f.at[0].add(carried)
    pooled_local = pooled_f.astype(jnp.bfloat16)
    key_part = jnp.dot(
        pooled_local, address_projection_coefficients, preferred_element_type=jnp.float32
    ).reshape(CAPL, -1, head_dim)
    value_part = jnp.dot(
        pooled_local, content_projection_coefficients, preferred_element_type=jnp.float32
    ).reshape(CAPL, -1, head_dim)
    kv_mine = lax.psum_scatter(
        jnp.concatenate([key_part, value_part], axis=2), "grp", scatter_dimension=1, tiled=True
    )
    key_block = rms_scale(kv_mine[..., :head_dim], address_rescale_factors).astype(jnp.bfloat16)
    value_block = kv_mine[..., head_dim:].astype(jnp.bfloat16)
    packed = jnp.concatenate([key_block, value_block], axis=2)
    kv_heads = packed.shape[1]
    live_rows = (slot_ids < accumulated_amount).astype(jnp.bfloat16)
    dec_normed = rms_scale(
        textside_token_vectors.astype(jnp.float32), textside_rescale_factors
    ).astype(jnp.bfloat16)
    query_proj = jnp.dot(
        dec_normed, probe_projection_coefficients, preferred_element_type=jnp.float32
    ).reshape(query_count, -1, head_dim)
    queries = (
        rms_scale(query_proj, probe_rescale_factors)
        .astype(jnp.bfloat16)
        .reshape(query_count, kv_heads, -1, head_dim)
    )
    numerator, denominator = attend_block(
        lax.all_gather(packed, "seq", axis=0, tiled=True),
        lax.all_gather(live_rows, "seq", axis=0, tiled=True),
        queries,
        head_dim,
    )
    attended = (numerator / denominator[..., None]).astype(jnp.bfloat16).reshape(query_count, -1)
    partial_out = jnp.dot(
        attended,
        lax.all_gather(mixing_exit_coefficients, "seq", axis=1, tiled=True),
        preferred_element_type=jnp.float32,
    )
    summed = lax.psum_scatter(partial_out, "grp", scatter_dimension=1, tiled=True)
    out_width = summed.shape[1]
    residual_dec = lax.dynamic_slice_in_dim(
        textside_token_vectors, grp_index * out_width, out_width, 1
    ).astype(jnp.float32)
    dec_out = (residual_dec + summed).astype(jnp.bfloat16)
    return (frames_out, pooled_local, dec_out)


def solution(mesh):
    in_specs = (
        P("seq", None),
        P(),
        P(None, None, "grp"),
        P(None, "grp"),
        P("grp"),
        P("grp", None),
        P("seq"),
        P("seq"),
        P("seq", None),
        P(),
        P(None, "grp"),
        P(),
        P("grp", None),
        P("grp", None),
        P(),
        P("grp", "seq"),
    )
    out_specs = (P("seq", "grp"), P("seq", "grp"), P("seq", "grp"))
    return jax.shard_map(local, mesh=mesh, in_specs=in_specs, out_specs=out_specs, check_vma=False)
```

profile of v0, /device:TPU:0, one launch (start us, length us, event | category | flops | bytes accessed | tf_op | source)
XLA Modules:
  0.0 329.2 jit_solution(172589755580196405)
XLA Ops:
  7.2 2.5 convert_reduce_fusion
  12.3 2.4 copy.44
  14.8 5.4 %fusion.2 = f32[1024,2,384]{2,0,1:T(8,128)S(1)} fusion(bf16[2,384,1536]{2,1,0:T(8,128)(2,1)} %bitcast.125, bf16[1024,1536]{1,0:T(8,128)(2,1)} %param.20, f32[1536]{0:T(1024)S(1)} %copy-done.11, f32[1024]{0:T(1024)S(1)} %add_rsqrt_fusion.2, f32[1024]{0:T(1024)S(1)} %broadcast_multiply_fusion.1), kind=kOutput, calls=%fused_computation.38 | convolution fusion | flops 2423783424 | bytes 8665088 | tf_op jit(solution)/shard_map/dot_general | solution.py:104
  20.6 2.4 collective-permute-start
  23.0 1.4 collective-permute-start.1
  25.1 3.3 %collective-permute-done.1 = bf16[15,384]{1,0:T(8,128)(2,1)S(1)} collective-permute-done((bf16[15,384]{1,0:T(8,128)(2,1)S(1)}, bf16[15,384]{1,0:T(8,128)(2,1)S(1)}, u32[]{:S(2)}, u32[]{:S(2)}) %collective-permute-start.1) | collective-permute-done | bytes 11552 | tf_op jit(solution)/shard_map/ppermute | solution.py:24
  28.4 11.1 %fusion.81 = (f32[1024]{0:T(1024)S(1)}, f32[1024]{0:T(1024)S(1)}, f32[1024,384]{1,0:T(8,128)S(1)}) fusion(bf16[15,384]{1,0:T(8,128)(2,1)S(1)} %collective-permute-done.1, bf16[1024,384]{1,0:T(8,128)(2,1)S(1)} %fusion.93, f32[384]{0:T(512)S(1)} %get-tuple-element.159, f32[384]{0:T(512)S(1)} %get-tuple-element.160, f32[384]{0:T(512)S(1)} %get-tuple-element.131, ...), kind=kLoop, calls=%fused_computation.195 | loop fusion | flops 72742912 | bytes 2438144 | tf_op jit(solution)/shard_map/reduce_sum | solution.py:119
  39.5 10.1 %all-reduce.2 = (f32[1024]{0:T(1024)S(1)}, f32[1024]{0:T(1024)S(1)}) all-reduce(f32[1024]{0:T(1024)S(1)} %get-tuple-element.129, f32[1024]{0:T(1024)S(1)} %get-tuple-element.128), channel_id=1, replica_groups=mesh['grp'=4,'seq'=8] {'grp'}, use_global_device_ids=true, to_apply=%region_5.0 | all-reduce | flops 2048 | bytes 16384 | tf_op jit(solution)/shard_map/psum | solution.py:118
  49.6 4.6 %fusion.37 = f32[1024,1536]{1,0:T(8,128)} fusion(bf16[384,1536]{1,0:T(8,128)(2,1)S(1)} %copy-done, f32[1024,384]{1,0:T(8,128)S(1)} %get-tuple-element.177, f32[384]{0:T(512)S(1)} %copy-done.12, f32[1024]{0:T(1024)S(1)} %get-tuple-element.181, f32[1024]{0:T(1024)S(1)} %get-tuple-element.180), kind=kOutput, calls=%fused_computation.75 | convolution fusion | flops 1211105280 | bytes 9053696 | tf_op jit(solution)/shard_map/dot_general | solution.py:130
  57.6 14.1 %all-reduce = f32[8]{0:T(128)S(1)} all-reduce(f32[8]{0:T(128)S(1)} %dynamic-update-slice.3), channel_id=1, replica_groups=mesh['grp'=4,'seq'=8] {'seq'}, use_global_device_ids=true, to_apply=%add | all-reduce | flops 8 | bytes 64
  71.6 5.4 %convert_element_type.157 = f32[1024,1536]{1,0:T(8,128)} convert(bf16[1024,1536]{1,0:T(8,128)(2,1)} %param.20) | non-fusion elementwise | flops 1572864 | bytes 9437184 | tf_op jit(solution)/shard_map/convert_element_type | solution.py:102
  78.9 45.7 %reduce-scatter.3.cloned.1.call-done = f32[1024,384]{1,0:T(8,128)} async-done(((f32[1024,1536]{1,0:T(8,128)}), f32[1024,384]{1,0:T(8,128)}) %reduce-scatter.3.cloned.1.call-update) | async-done | bytes 1572880 | tf_op jit(solution)/shard_map/reduce_scatter | solution.py:129
  124.6 2.2 multiply_reduce_fusion.1
  126.8 13.0 %all-gather.1 = f32[8,1,384]{2,1,0:T(1,128)S(1)} all-gather(f32[1,1,384]{2,1,0:T(1,128)S(1)} %reshape.175), channel_id=2, replica_groups=mesh['grp'=4,'seq'=8] {'seq'}, dimensions={0}, use_global_device_ids=true | all-gather | bytes 13824 | tf_op jit(solution)/shard_map/all_gather | solution.py:33
  139.8 10.0 %while.15 = (s32[]{:T(128)}, f32[384]{0:T(512)S(1)}, s32[]{:T(128)}, f32[8]{0:T(128)S(1)}, f32[8,384]{1,0:T(8,128)S(1)}, /*index=5*/s32[]{:T(128)}, s32[]{:T(128)}, f32[1]{0:T(128)}) while((s32[]{:T(128)}, f32[384]{0:T(512)S(1)}, s32[]{:T(128)}, f32[8]{0:T(128)S(1)}, f32[8,384]{1,0:T(8,128)S(1)}, /*index=5*/s32[]{:T(128)}, ...), condition=%wide.region_12.13_spmd.clone, body=%wide.region_11.12_spmd.clone.sunk | while | flops 1541 | bytes 7811 | solution.py:42
  149.8 1.3 fusion.20
  151.2 1.4 convolution_bitcast_fusion
  152.6 1.3 convolution_bitcast_fusion.1
  154.0 1.1 pad_maximum_fusion
  155.8 50.7 %all-reduce.5.cloned.1.call-done = f32[256,4,256]{2,0,1:T(8,128)} async-done(((f32[256,4,256]{2,0,1:T(8,128)}), f32[256,4,256]{2,0,1:T(8,128)}) %all-reduce.5.cloned.1.call-update) | async-done | bytes 1048592
  206.4 1.7 multiply_reduce_fusion.3
  208.1 1.6 dynamic-slice_convert_fusion
  209.8 1.6 multiply_convert_fusion.3
  213.4 11.8 %all-gather.2 = bf16[8,1,256]{2,1,0:T(2,128)(2,1)S(1)} all-gather(bf16[1,1,256]{2,1,0:T(2,128)(2,1)S(1)} %reshape.177), channel_id=1, replica_groups=mesh['grp'=4,'seq'=8] {'seq'}, dimensions={0}, use_global_device_ids=true | all-gather | bytes 4608 | tf_op jit(solution)/shard_map/all_gather | solution.py:182
  225.3 1.6 fusion.7
  226.9 3.3 fusion.82
  230.5 3.9 %all-gather.6.cloned.1.call-done = bf16[2048,1,256]{2,0,1:T(8,128)(2,1)} async-done(((bf16[256,1,256]{2,0,1:T(8,128)(2,1)}), bf16[2048,1,256]{2,0,1:T(8,128)(2,1)}) %all-gather.6.cloned.1.call-update) | async-done | bytes 1048592 | tf_op jit(solution)/shard_map/all_gather | solution.py:181
  234.6 2.0 bitcast_reduce_fusion
  237.6 44.8 %all-gather.8.cloned.1.call-done = bf16[512,4096]{1,0:T(8,128)(2,1)} async-done(((bf16[512,512]{1,0:T(8,128)(2,1)}), bf16[512,4096]{1,0:T(8,128)(2,1)}) %all-gather.8.cloned.1.call-update) | async-done | bytes 4194320 | tf_op jit(solution)/shard_map/all_gather | solution.py:189
  282.4 4.3 %fusion.83 = f32[128,4096]{1,0:T(8,128)} fusion(bf16[128,512]{0,1:T(8,128)(2,1)S(1)} %bitcast.127, bf16[512,4096]{1,0:T(8,128)(2,1)} %all-gather.8.cloned.1.call-done), kind=kOutput, calls=%fused_computation.197 | convolution fusion | flops 536870912 | bytes 6422528 | tf_op jit(solution)/shard_map/dot_general | solution.py:187
  287.6 33.2 %reduce-scatter.5.cloned.1.call-done = f32[128,1024]{1,0:T(8,128)} async-done(((f32[128,4096]{1,0:T(8,128)}), f32[128,1024]{1,0:T(8,128)}) %reduce-scatter.5.cloned.1.call-update) | async-done | bytes 524304 | tf_op jit(solution)/shard_map/reduce_scatter | solution.py:192
  320.8 1.9 add_convert_fusion
  (103 shorter events, 18.4 us)
Async XLA Ops:
  7.2 42.4 %copy-start = (bf16[384,1536]{1,0:T(8,128)(2,1)S(1)}, bf16[384,1536]{1,0:T(8,128)(2,1)}, u32[]{:S(2)}) copy-start(bf16[384,1536]{1,0:T(8,128)(2,1)} %param.25) | copy-start | bytes 3538948
  7.2 117.4 %reduce-scatter.3.cloned.1.call-start = ((), (), s32[]{:S(2)}) async-start(), calls=%async_computation.2 | async-start | bytes 7864320 | tf_op jit(solution)/shard_map/reduce_scatter | solution.py:129
  7.2 2.9 copy-start.1
  10.1 1.7 copy-start.2
  12.3 2.5 copy-start.11
  20.6 4.5 %collective-permute-start = (bf16[15,384]{1,0:T(8,128)(2,1)S(1)}, bf16[15,384]{1,0:T(8,128)(2,1)S(1)}, u32[]{:S(2)}, u32[]{:S(2)}) collective-permute-start(bf16[15,384]{1,0:T(8,128)(2,1)S(1)} %get-tuple-element.178), channel_id=1, source_target_pairs={{0,1},{1,2},{2,3},{3,4},{4,5},{5,6},{6,7},{8,9},{9,10},{10,11},{11... | collective-permute-start | bytes 34568 | tf_op jit(solution)/shard_map/ppermute | solution.py:22
  23.0 1.9 copy-start.5
  23.0 5.4 %collective-permute-start.1 = (bf16[15,384]{1,0:T(8,128)(2,1)S(1)}, bf16[15,384]{1,0:T(8,128)(2,1)S(1)}, u32[]{:S(2)}, u32[]{:S(2)}) collective-permute-start(bf16[15,384]{1,0:T(8,128)(2,1)S(1)} %get-tuple-element.179), channel_id=1, source_target_pairs={{1,0},{2,1},{3,2},{4,3},{5,4},{6,5},{7,6},{9,8},{10,9},{11,10},{12... | collective-permute-start | bytes 34568 | tf_op jit(solution)/shard_map/ppermute | solution.py:24
  24.9 24.7 %copy-start.12 = (f32[384]{0:T(512)S(1)}, f32[384]{0:T(512)}, u32[]{:S(2)}) copy-start(f32[384]{0:T(512)} %param.24) | copy-start | bytes 4612
  54.2 0.7 copy-start.6
  54.2 2.0 copy-start.14
  54.3 152.2 %all-reduce.5.cloned.1.call-start = ((), (), s32[]{:S(2)}) async-start(), calls=%async_computation.6 | async-start | bytes 2097152
  71.6 53.0 %copy-start.8 = (f32[1024]{0:T(1024)S(1)}, f32[1024]{0:T(1024)}, u32[]{:S(2)}) copy-start(f32[1024]{0:T(1024)} %param.26) | copy-start | bytes 12292
  151.2 2.7 copy-start.3
  154.0 1.2 copy-start.13
  154.0 55.8 %copy-start.9 = (f32[128]{0:T(128)S(1)}, f32[128]{0:T(128)}, u32[]{:S(2)}) copy-start(f32[128]{0:T(128)} %param.34) | copy-start | bytes 1540
  155.1 71.7 %copy-start.7 = (f32[4096]{0:T(1024)S(1)}, f32[4096]{0:T(1024)}, u32[]{:S(2)}) copy-start(f32[4096]{0:T(1024)} %param.29) | copy-start | bytes 49156
  155.1 79.2 %all-gather.6.cloned.1.call-start = ((), (), s32[]{:S(2)}) async-start(), calls=%async_computation.3 | async-start | bytes 1179648 | tf_op jit(solution)/shard_map/all_gather | solution.py:181
  212.1 70.3 %all-gather.8.cloned.1.call-start = ((), (), s32[]{:S(2)}) async-start(), calls=%async_computation.4 | async-start | bytes 4718592 | tf_op jit(solution)/shard_map/all_gather | solution.py:189
  212.7 108.1 %reduce-scatter.5.cloned.1.call-start = ((), (), s32[]{:S(2)}) async-start(), calls=%async_computation.5 | async-start | bytes 2621440 | tf_op jit(solution)/shard_map/reduce_scatter | solution.py:192
  226.8 3.6 %copy-start.10 = (f32[128]{0:T(128)S(1)}, f32[128]{0:T(128)}, u32[]{:S(2)}) copy-start(f32[128]{0:T(128)} %param.31) | copy-start | bytes 1540
  234.6 2.0 copy-start.4
Sparse Core Ops, SparseCore 0:
  54.4 70.1 reduce-scatter.2
  155.3 51.1 all-reduce.4
  212.2 22.0 all-gather.5
  235.8 46.5 all-gather.7
  286.8 33.9 reduce-scatter.4
where the time goes:
time: 330 us; the launch traced here: 329 us
  waiting for transfers between devices  182 us (55%)
  blocking collectives  48.9 us (15%)
  other arithmetic  35.9 us (11%)
  matrix products  24.6 us (7%)
  between operations  14.9 us (5%)
  local copies, waits for them, and re-layouts  13.9 us (4%)
  loops' own time  5.02 us (2%)
  starting transfers between devices  4.02 us (1%)
    unnamed x6, waiting for transfers between devices  51.2 us
    reduce_scatter x1, waiting for transfers between devices, local(): lax.psum_scatter(jnp.dot(activated, unitwise_exit_coefficients, preferred...  45.7 us
    all_gather x1, waiting for transfers between devices, local(): lax.all_gather(mixing_exit_coefficients, 'seq', axis=1, tiled=True)  44.8 us
    reduce_scatter x1, waiting for transfers between devices, local(): lax.psum_scatter(partial_out, 'grp', scatter_dimension=1, tiled=True)  33.2 us
    unnamed x1, blocking collectives  14.1 us
    all_gather x1, blocking collectives, entering(): pieces = jax.tree.map(lambda part: lax.all_gather(part, axis), value)  13 us
    all_gather x1, blocking collectives, local(): lax.all_gather(live_rows, 'seq', axis=0, tiled=True)  11.8 us
    reduce_sum x1, other arithmetic, local(): jnp.sum(mixed_conv, axis=1)  11.1 us
  transfers between devices with their start and end apart: 7, of which 6 were waited for; matrix products, arithmetic and copies ran while one was open for 6% of the time, Pallas kernels for 0%

commit v1 on v0

v1 whole, which is shorter than its diff:
```python
import functools

import jax
import jax.numpy as jnp
from jax import lax
from jax.experimental import pallas as pl
from jax.experimental.pallas import tpu as pltpu
from jax.sharding import PartitionSpec as P

CAPL = 256
EPS_LAYER = 1e-05
EPS_ROOT = 1e-06
SCORE_SCALE = 0.25
RIM = 16
MESH = pl.DeviceIdType.MESH


def exchange_kernel(axis, n, routes, *refs):
    m = len(routes)
    xs, outs = refs[:m], refs[m : 2 * m]
    send, recv, own = refs[2 * m :]
    me = lax.axis_index(axis)
    barrier = pltpu.get_barrier_semaphore()
    for k in range(1, n):
        pl.semaphore_signal(
            barrier, inc=1, device_id={axis: lax.rem(me + k, n)}, device_id_type=MESH
        )
    pl.semaphore_wait(barrier, n - 1)
    copies = []
    for i, (take, put) in enumerate(routes):
        for k in range(1, n):
            peer = lax.rem(me + k, n)
            copy = pltpu.make_async_remote_copy(
                src_ref=take(xs[i], peer),
                dst_ref=put(outs[i], me),
                send_sem=send.at[i, k],
                recv_sem=recv.at[i, k],
                device_id={axis: peer},
                device_id_type=MESH,
            )
            copy.start()
            copies.append(copy)
        mine = pltpu.make_async_copy(take(xs[i], me), put(outs[i], me), own.at[i])
        mine.start()
        copies.append(mine)
    for copy in copies:
        copy.wait()


def exchange(arrays, shapes, routes, axis, collective_id, name):
    n = lax.axis_size(axis)
    m = len(arrays)
    vmem = pl.BlockSpec(memory_space=pltpu.VMEM)
    return pl.pallas_call(
        functools.partial(exchange_kernel, axis, n, routes),
        out_shape=[jax.ShapeDtypeStruct(s, a.dtype) for s, a in zip(shapes, arrays)],
        in_specs=[vmem] * m,
        out_specs=[vmem] * m,
        scratch_shapes=[
            pltpu.SemaphoreType.DMA((m, n)),
            pltpu.SemaphoreType.DMA((m, n)),
            pltpu.SemaphoreType.DMA((m,)),
        ],
        compiler_params=pltpu.CompilerParams(
            collective_id=collective_id, has_side_effects=True
        ),
        name=name,
    )(*arrays)


def rows_at(size, length=None):
    length = length or size
    return lambda ref, i: ref.at[pl.ds(pl.multiple_of(i * size, size), length), :]


def cols_at(size):
    return lambda ref, i: ref.at[:, pl.ds(pl.multiple_of(i * size, size), size)]


def whole(ref, i):
    return ref


def slab(ref, i):
    return ref.at[i]


def gather_pairs_kernel(axis, n, x_ref, o_ref, send, recv, mate_send, mate_recv, own):
    rows = x_ref.shape[0]
    half = n // 2
    me = lax.axis_index(axis)
    mate = me + 1 - 2 * lax.rem(me, 2)

    def place(i):
        return o_ref.at[pl.ds(pl.multiple_of(i * rows, rows), rows), :]

    barrier = pltpu.get_barrier_semaphore()
    for k in range(1, half):
        pl.semaphore_signal(
            barrier, inc=1, device_id={axis: lax.rem(me + 2 * k, n)}, device_id_type=MESH
        )
    pl.semaphore_signal(barrier, inc=1, device_id={axis: mate}, device_id_type=MESH)
    pl.semaphore_wait(barrier, half)

    def over(src, dst, s, r, device):
        return pltpu.make_async_remote_copy(
            src_ref=src, dst_ref=dst, send_sem=s, recv_sem=r,
            device_id={axis: device}, device_id_type=MESH,
        )

    copies, forwards = [], []
    for k in range(1, half):
        copy = over(x_ref, place(me), send.at[k], recv.at[k], lax.rem(me + 2 * k, n))
        copy.start()
        copies.append(copy)
    first = over(x_ref, place(me), mate_send.at[0], mate_recv.at[0], mate)
    first.start()
    forwards.append(first)
    mine = pltpu.make_async_copy(x_ref, place(me), own)
    mine.start()
    for k in range(1, half):
        copies[k - 1].wait_recv()
        origin = lax.rem(me + n - 2 * k, n)
        hand = over(place(origin), place(origin), mate_send.at[k], mate_recv.at[k], mate)
        hand.start()
        forwards.append(hand)
    for hand in forwards:
        hand.wait()
    for copy in copies:
        copy.wait_send()
    mine.wait()


def gather_pairs(x, axis, collective_id, name):
    n = lax.axis_size(axis)
    vmem = pl.BlockSpec(memory_space=pltpu.VMEM)
    half = n // 2
    dma = pltpu.SemaphoreType.DMA
    return pl.pallas_call(
        functools.partial(gather_pairs_kernel, axis, n),
        out_shape=jax.ShapeDtypeStruct((n * x.shape[0], x.shape[1]), x.dtype),
        in_specs=[vmem],
        out_specs=vmem,
        scratch_shapes=[dma((half,)), dma((half,)), dma((half,)), dma((half,)), dma(())],
        compiler_params=pltpu.CompilerParams(
            collective_id=collective_id, has_side_effects=True
        ),
        name=name,
    )(x)


def layer_norm(inputs, scales):
    center = jnp.mean(inputs, axis=-1, keepdims=True)
    variance = jnp.mean((inputs - center) * (inputs - center), axis=-1, keepdims=True)
    return (inputs - center) * lax.rsqrt(variance + EPS_LAYER) * scales


def rms_scale(inputs, scales):
    return inputs * lax.rsqrt(jnp.mean(inputs * inputs, axis=-1, keepdims=True) + EPS_ROOT) * scales


def local(
    acoustic_sequence,
    entry_rescale_factors,
    unitwise_entry_coefficients,
    channelwise_filter_taps,
    filtering_rescale_factors,
    unitwise_exit_coefficients,
    accumulation_coefficients,
    spike_indicator,
    textside_token_vectors,
    textside_rescale_factors,
    probe_projection_coefficients,
    probe_rescale_factors,
    address_projection_coefficients,
    content_projection_coefficients,
    address_rescale_factors,
    mixing_exit_coefficients,
):
    frame_count, feature_width = acoustic_sequence.shape
    columns = unitwise_entry_coefficients.shape[2]
    groups = lax.axis_size("grp")
    blocks = lax.axis_size("seq")
    grp_index = lax.axis_index("grp")
    head_dim = probe_rescale_factors.shape[0]
    query_count, text_width = textside_token_vectors.shape
    share = frame_count // groups
    tap_total = channelwise_filter_taps.shape[0]
    f32, bf16 = jnp.float32, jnp.bfloat16

    exit_all = lax.all_gather(unitwise_exit_coefficients, "grp", axis=0, tiled=True)
    mixing_all = lax.all_gather(mixing_exit_coefficients, "seq", axis=1, tiled=True)

    before = lax.ppermute(
        acoustic_sequence[frame_count - RIM :], "seq", [(i, i + 1) for i in range(blocks - 1)]
    )
    after = lax.ppermute(
        acoustic_sequence[:RIM], "seq", [(i + 1, i) for i in range(blocks - 1)]
    )
    entry = unitwise_entry_coefficients.reshape(feature_width, 2 * columns)

    def gate(frames):
        normed = layer_norm(frames.astype(f32), entry_rescale_factors).astype(bf16)
        projected = jnp.dot(normed, entry, preferred_element_type=f32)
        return (projected[:, :columns] * jax.nn.sigmoid(projected[:, columns:])).astype(bf16)

    rims = gate(jnp.concatenate([before, after], axis=0))
    widened = jnp.concatenate([rims[:RIM], gate(acoustic_sequence), rims[RIM:]], axis=0)
    packed_taps = jnp.concatenate(
        [channelwise_filter_taps, filtering_rescale_factors[None, :]], axis=0
    )
    strip = share + 2 * RIM
    strips, taps_all = exchange(
        [widened, packed_taps],
        [(strip, feature_width), (tap_total + 1, feature_width)],
        [(rows_at(share, strip), cols_at(columns)), (whole, cols_at(columns))],
        "grp",
        1,
        "to_frames",
    )

    strips_f = strips.astype(f32)
    shift = RIM - tap_total // 2
    mixed_conv = jnp.zeros((share, feature_width), f32)
    for tap_index in range(tap_total):
        mixed_conv = mixed_conv + taps_all[tap_index] * strips_f[
            tap_index + shift : tap_index + shift + share
        ]
    normal_part = layer_norm(mixed_conv, taps_all[tap_total])
    activated = (normal_part * jax.nn.sigmoid(normal_part)).astype(bf16)
    residual_part = lax.dynamic_slice_in_dim(acoustic_sequence, grp_index * share, share, 0)
    hidden = (
        residual_part.astype(f32) + jnp.dot(activated, exit_all, preferred_element_type=f32)
    ).astype(bf16)
    (frames_out,) = exchange(
        [hidden],
        [(frame_count, columns)],
        [(cols_at(columns), rows_at(share))],
        "grp",
        2,
        "to_channels",
    )

    prior = jnp.cumsum(spike_indicator) - spike_indicator
    fired = jnp.sum(spike_indicator)
    weighted = accumulation_coefficients[:, None] * frames_out.astype(f32)
    slot_ids = jnp.arange(CAPL, dtype=jnp.int32)
    selector = (slot_ids[:, None] == prior[None, :]).astype(f32)
    sums = jnp.dot(selector, weighted, precision=lax.Precision.HIGHEST)
    tail_sum = lax.dynamic_slice_in_dim(sums, fired, 1, 0)
    carried = lax.ppermute(tail_sum, "seq", [(i, i + 1) for i in range(blocks - 1)])
    live = slot_ids[:, None] < fired
    pooled_local = jnp.where(
        live, sums + jnp.where(slot_ids[:, None] == 0, carried, 0.0), 0.0
    ).astype(bf16)

    kv_heads = address_projection_coefficients.shape[1] // head_dim
    key_part = jnp.dot(
        pooled_local, address_projection_coefficients, preferred_element_type=f32
    ).astype(bf16)
    value_part = jnp.dot(
        pooled_local, content_projection_coefficients, preferred_element_type=f32
    ).astype(bf16)
    (kv_parts,) = exchange(
        [jnp.stack([key_part, value_part])],
        [(groups, 2, CAPL, head_dim)],
        [
            (
                lambda ref, i: ref.at[
                    :, :, pl.ds(pl.multiple_of(i * head_dim, head_dim), head_dim)
                ],
                slab,
            )
        ],
        "grp",
        3,
        "kv_heads",
    )
    kv_mine = jnp.sum(kv_parts.astype(f32), axis=0)
    key_block = rms_scale(kv_mine[0], address_rescale_factors).astype(bf16)
    value_block = kv_mine[1].astype(bf16)
    note = jnp.concatenate(
        [jnp.zeros((16, head_dim), bf16), jnp.full((16, head_dim), fired, bf16)], axis=1
    )
    packed = jnp.concatenate(
        [jnp.concatenate([key_block, value_block], axis=1), note], axis=0
    )
    everyone = gather_pairs(packed, "seq", 4, "kv_rows")
    rows = CAPL + 16
    counts = everyone.reshape(blocks, rows, 2 * head_dim)[:, CAPL, head_dim]
    live_all = (
        jnp.arange(rows, dtype=jnp.int32)[None, :] < counts.astype(jnp.int32)[:, None]
    ).reshape(blocks * rows)

    dec_normed = rms_scale(
        textside_token_vectors.astype(f32), textside_rescale_factors
    ).astype(bf16)
    query_proj = jnp.dot(
        dec_normed, probe_projection_coefficients, preferred_element_type=f32
    ).reshape(query_count, -1, head_dim)
    queries = rms_scale(query_proj, probe_rescale_factors).astype(bf16)
    heads = queries.shape[1]
    queries = queries.transpose(1, 0, 2).reshape(heads * query_count, head_dim)
    scores = (
        lax.dot_general(
            queries, everyone[:, :head_dim], (((1,), (1,)), ((), ())), preferred_element_type=f32
        )
        * SCORE_SCALE
    )
    weights = jnp.where(live_all[None, :], jnp.exp(scores), 0.0)
    numerator = jnp.dot(
        weights.astype(bf16), everyone[:, head_dim:], preferred_element_type=f32
    )
    denominator = jnp.sum(weights, axis=-1, keepdims=True)
    attended = (
        (numerator / denominator)
        .astype(bf16)
        .reshape(heads, query_count, head_dim)
        .transpose(1, 0, 2)
        .reshape(query_count, heads * head_dim)
    )
    partial_out = jnp.dot(attended, mixing_all, preferred_element_type=f32).astype(bf16)
    out_width = text_width // groups
    (parts,) = exchange(
        [partial_out],
        [(groups, query_count, out_width)],
        [(cols_at(out_width), slab)],
        "grp",
        5,
        "dec_sums",
    )
    residual_dec = lax.dynamic_slice_in_dim(
        textside_token_vectors, grp_index * out_width, out_width, 1
    ).astype(f32)
    dec_out = (residual_dec + jnp.sum(parts.astype(f32), axis=0)).astype(bf16)
    return (frames_out, pooled_local, dec_out)


def solution(mesh):
    in_specs = (
        P("seq", None),
        P(),
        P(None, None, "grp"),
        P(None, "grp"),
        P("grp"),
        P("grp", None),
        P("seq"),
        P("seq"),
        P("seq", None),
        P(),
        P(None, "grp"),
        P(),
        P("grp", None),
        P("grp", None),
        P(),
        P("grp", "seq"),
    )
    out_specs = (P("seq", "grp"), P("seq", "grp"), P("seq", "grp"))
    return jax.shard_map(local, mesh=mesh, in_specs=in_specs, out_specs=out_specs, check_vma=False)
```

time: 330 us -> 188 us (0.57)
  waiting for transfers between devices: 182 us -> 0.75 us
  Pallas kernels: 0 us -> 92.7 us
  blocking collectives: 48.9 us -> 0 us
  loops' own time: 5.02 us -> 0 us
    pallas_call x0 -> x5, Pallas kernels: none -> 92.7 us  [the longest x4 75 us: exchange(): pl.pallas_call(functools.partial(exchange_kernel, axis, n, routes), out_s...]
    reduce_scatter x2 -> x0, waiting for transfers between devices: 78.8 us -> none  [the longest x1 45.7 us: local(): lax.psum_scatter(jnp.dot(activated, unitwise_exit_coefficients, preferred...]
    unnamed x6 -> x2, waiting for transfers between devices: 51.2 us -> 0.7 us
    all_gather x1, waiting for transfers between devices: 44.8 us -> 0.02 us  [local(): lax.all_gather(mixing_exit_coefficients, 'seq', axis=1, tiled=True)]
    all_gather x2 -> x0, blocking collectives: 24.8 us -> none  [the longest x1 13 us: entering(): pieces = jax.tree.map(lambda part: lax.all_gather(part, axis), value)]
    unnamed x1 -> x0, blocking collectives: 14.1 us -> none
    psum x1 -> x0, blocking collectives: 10.1 us -> none  [local(): lax.psum((jnp.sum(mixed_conv, axis=1), jnp.sum(mixed_conv * mixed_conv, a...]
    reduce_sum x3, other arithmetic: 13.9 us -> 4.73 us  [the longest x1 2.03 us: local(): fired = jnp.sum(spike_indicator)]
  transfers between devices with their start and end apart: 7 -> 5, of which waited for: 6 -> 0; matrix products, arithmetic and copies ran while one was open for 6% -> 31% of each run, Pallas kernels for 0% -> 40%
where the time goes in v1:
time: 188 us; the launch traced here: 187 us
  Pallas kernels  92.7 us (49%)
  other arithmetic  33.6 us (18%)
  matrix products  24.7 us (13%)
  between operations  17.1 us (9%)
  local copies, waits for them, and re-layouts  11.5 us (6%)
  starting transfers between devices  6.41 us (3%)
    pallas_call x4, Pallas kernels, exchange(): pl.pallas_call(functools.partial(exchange_kernel, axis, n, routes), out_s...  75 us
    pallas_call x1, Pallas kernels, gather_pairs(): pl.pallas_call(functools.partial(gather_pairs_kernel, axis, n), out_shape...  17.6 us
    reduce_sum x3, other arithmetic, layer_norm(): center = jnp.mean(inputs, axis=-1, keepdims=True)  11.6 us
    dot_general x1, matrix products, local(): jnp.dot(activated, exit_all, preferred_element_type=f32)  5.54 us
    dot_general x2, matrix products, gate(): projected = jnp.dot(normed, entry, preferred_element_type=f32)  5.08 us
    unnamed x43, local copies, waits for them, and re-layouts  5.08 us
    dot_general x1, matrix products, local(): jnp.dot(dec_normed, probe_projection_coefficients, preferred_element_type...  3.99 us
    dot_general x1, matrix products, local(): jnp.dot(attended, mixing_all, preferred_element_type=f32).astype(bf16)  3.93 us
  transfers between devices with their start and end apart: 5, of which 0 were waited for; matrix products, arithmetic and copies ran while one was open for 31% of the time, Pallas kernels for 40%

profile of v1, /device:TPU:0, one launch (start us, length us, event | category | flops | bytes accessed | tf_op | source)
XLA Modules:
  0.0 186.6 jit_solution(11403043553639966441)
XLA Ops:
  8.0 1.5 fusion.98
  9.4 3.0 %collective-permute-start = (bf16[16,1536]{1,0:T(8,128)(2,1)}, bf16[16,1536]{1,0:T(8,128)(2,1)}, u32[]{:S(2)}, u32[]{:S(2)}) collective-permute-start(bf16[16,1536]{1,0:T(8,128)(2,1)} %get-tuple-element.41), channel_id=1, source_target_pairs={{0,1},{1,2},{2,3},{3,4},{4,5},{5,6},{6,7},{8,9},{9,10},{10,11},{11... | collective-permute-start | bytes 147464 | tf_op jit(solution)/shard_map/ppermute | solution.py:194
  12.4 1.3 collective-permute-start.1
  13.7 2.5 %convert_reduce_fusion = f32[1024]{0:T(1024)S(1)} fusion(bf16[1024,1536]{1,0:T(8,128)(2,1)} %param.16), kind=kLoop, calls=%fused_computation.1 | loop fusion | flops 3144704 | bytes 3149824 | tf_op jit(solution)/shard_map/reduce_sum | solution.py:153
  16.9 2.3 %copy-done.1 = bf16[1024,1536]{1,0:T(8,128)(2,1)S(1)} copy-done((bf16[1024,1536]{1,0:T(8,128)(2,1)S(1)}, bf16[1024,1536]{1,0:T(8,128)(2,1)}, u32[]{:S(2)}) %copy-start.1) | copy-done | bytes 3145752
  20.1 2.8 %fusion.7 = f32[1024,768]{1,0:T(8,128)S(1)} fusion(bf16[1536,768]{1,0:T(8,128)(2,1)S(1)} %bitcast.49, bf16[1024,1536]{1,0:T(8,128)(2,1)S(1)} %copy-done.1, f32[1536]{0:T(1024)S(1)} %copy-done.13, f32[1024]{0:T(1024)S(1)} %add_rsqrt_fusion, f32[1024]{0:T(1024)S(1)} %broadcast_multiply_fusion), kind=kOutput, calls=%fused_computation.11 | convolution fusion | flops 2423783424 | bytes 8665088 | tf_op jit(solution)/shard_map/dot_general | solution.py:204
  23.0 1.3 fusion.55
  25.4 2.0 %fusion.100 = (s32[]{:T(128)}, s32[1024]{0:T(1024)}) fusion(s32[1024]{0:T(1024)} %param.23, s32[8,128]{1,0:T(8,128)S(1)} %reduce-window.9, s32[8]{0:T(128)S(1)} %slice_reduce_fusion.32), kind=kLoop, calls=%fused_computation.202 | loop fusion | flops 3071 | bytes 12324 | tf_op jit(solution)/shard_map/reduce_sum | solution.py:245
  27.4 1.5 fusion.15
  28.9 4.0 %fusion.64 = f32[128,512]{1,0:T(8,128)} fusion(bf16[4096,512]{1,0:T(8,128)(2,1)} %param.26, bf16[128,4096]{1,0:T(8,128)(2,1)} %param.24, f32[4096]{0:T(1024)} %param.25, f32[128]{0:T(128)S(1)} %add_rsqrt_fusion.4), kind=kOutput, calls=%fused_computation.103 | convolution fusion | flops 538968064 | bytes 5521920 | tf_op jit(solution)/shard_map/dot_general | solution.py:298
  32.9 1.7 reshape.141
  34.7 1.8 multiply_reduce_fusion.1
  37.4 1.8 fusion.77
  39.1 1.4 pad_maximum_fusion.4.refs_1_
  42.5 1.1 convert_reduce_fusion.3
  44.6 2.3 %fusion.83 = f32[32,768]{1,0:T(8,128)S(1)} fusion(bf16[1536,768]{1,0:T(8,128)(2,1)} %bitcast.50, f32[1536]{0:T(1024)S(1)} %copy-done.14, f32[32]{0:T(128)S(1)} %add_rsqrt_fusion.5, f32[32]{0:T(128)S(1)} %broadcast_multiply_fusion.2, bf16[16,1536]{1,0:T(8,128)(2,1)} %collective-permute-done.1, bf16[16,1536]{1,0:T(8,128)(2,1)} %collective-permute-done), kind=kOutput, calls=%fused_computation.136 | convolution fusion | flops 75890688 | bytes 2562304 | tf_op jit(solution)/shard_map/dot_general | solution.py:204
  47.9 30.7 %to_frames.1 = (bf16[288,1536]{1,0:T(8,128)(2,1)}, f32[32,1536]{1,0:T(8,128)}) custom-call(bf16[1056,384]{1,0:T(8,128)(2,1)} %pad_maximum_fusion.refs_0_, f32[32,384]{1,0:T(8,128)} %pad_maximum_fusion.4.refs_1_), custom_call_target="tpu_custom_call" | custom-call | tf_op jit(solution)/shard_map/to_frames/pallas_call | solution.py:54
  78.6 1.4 convert_element_type.100
  80.6 8.1 %fusion.96 = (f32[256]{0:T(256)S(1)}, f32[256,1536]{1,0:T(8,128)S(1)}) fusion(f32[288,1536]{1,0:T(8,128)S(1)} %convert_element_type.100, f32[1536]{0:T(1024)S(1)} %get-tuple-element.8, f32[1536]{0:T(1024)S(1)} %get-tuple-element.9, f32[1536]{0:T(1024)S(1)} %get-tuple-element.10, f32[1536]{0:T(1024)S(1)} %get-tuple-element.11, ...), kind=kLoop, calls=%fused_computation.199 | loop fusion | flops 24379136 | bytes 50523136 | tf_op jit(solution)/shard_map/reduce_sum | solution.py:153
  88.7 1.2 copy-done.3
  90.2 5.5 %fusion.12.refs_0_ = bf16[256,1536]{1,0:T(8,128)(2,1)} fusion(bf16[1536,1536]{1,0:T(8,128)(2,1)} %all-gather.3.cloned.1.call-done, f32[256,1536]{1,0:T(8,128)} %copy-done.3, f32[1536]{0:T(1024)S(1)} %get-tuple-element.7, f32[256]{0:T(256)S(1)} %add_rsqrt_fusion.3, f32[256]{0:T(256)S(1)} %broadcast_multiply_fusion.1, bf16[1024,1536]{1,0:T(8,128)(2,1)S(1)} %copy-done.1, ...), kind=kOutput, calls=%fused_computation.18 | convolution fusion | flops 1212284928 | bytes 7872516 | tf_op jit(solution)/shard_map/dot_general | solution.py:233
  95.7 15.1 %to_channels.1 = bf16[1024,384]{1,0:T(8,128)(2,1)} custom-call(bf16[256,1536]{1,0:T(8,128)(2,1)} %fusion.12.refs_0_), custom_call_target="tpu_custom_call" | custom-call | tf_op jit(solution)/shard_map/to_channels/pallas_call | solution.py:54
  110.8 2.5 %fusion.52 = f32[256,384]{1,0:T(8,128)S(1)} fusion(bf16[1024,384]{1,0:T(8,128)(2,1)} %to_channels.1, f32[1024]{0:T(1024)S(1)} %copy-done.19, s32[1024]{0:T(1024)S(1)} %copy-done.16), kind=kOutput, calls=%fused_computation.91 | convolution fusion | flops 1209008128 | bytes 1187840 | tf_op jit(solution)/shard_map/dot_general | solution.py:249
  113.4 2.1 %collective-permute-start.2 = (f32[1,384]{1,0:T(1,128)S(1)}, f32[1,384]{1,0:T(1,128)S(1)}, u32[]{:S(2)}, u32[]{:S(2)}) collective-permute-start(f32[1,384]{1,0:T(1,128)S(1)} %constant_dynamic-slice_fusion), channel_id=1, source_target_pairs={{0,1},{1,2},{2,3},{3,4},{4,5},{5,6},{6,7},{8,9},{9,10},{10,11},{11... | collective-permute-start | bytes 4616 | tf_op jit(solution)/shard_map/ppermute | solution.py:251
  118.4 11.8 %kv_heads.1 = bf16[4,2,256,128]{3,2,1,0:T(8,128)(2,1)} custom-call(bf16[2,256,512]{2,1,0:T(8,128)(2,1)} %pad_maximum_fusion.1.refs_0_), custom_call_target="tpu_custom_call" | custom-call | tf_op jit(solution)/shard_map/kv_heads/pallas_call | solution.py:54
  130.2 1.2 convert_reduce_fusion.2
  132.4 17.6 %kv_rows.1 = bf16[2176,256]{1,0:T(8,128)(2,1)} custom-call(bf16[272,256]{1,0:T(8,128)(2,1)} %pad_maximum_fusion.2.x_ref), custom_call_target="tpu_custom_call" | custom-call | tf_op jit(solution)/shard_map/kv_rows/pallas_call | solution.py:139
  151.0 2.3 %fusion.101 = (f32[512]{0:T(512)S(1)}, bf16[512,2176]{1,0:T(8,128)(2,1)S(1)}) fusion(bf16[512,128]{1,0:T(8,128)(2,1)S(1)} %bitcast.54, bf16[2176,256]{1,0:T(8,128)(2,1)} %kv_rows.1, pred[2176]{0:T(1024)(128)(4,1)S(1)} %lt.48), kind=kOutput, calls=%fused_computation.203 | convolution fusion | flops 289668608 | bytes 2920576 | tf_op jit(solution)/shard_map/dot_general | solution.py:305
  154.2 3.9 %convolution_convert_fusion.refs_0_ = bf16[128,4096]{1,0:T(8,128)(2,1)} fusion(bf16[128,512]{0,1:T(8,128)(2,1)S(1)} %bitcast.53, bf16[512,4096]{1,0:T(8,128)(2,1)} %all-gather.5.cloned.1.call-done), kind=kOutput, calls=%fused_computation.10 | convolution fusion | flops 537395200 | bytes 5373952 | tf_op jit(solution)/shard_map/dot_general | solution.py:322
  158.2 17.5 %dec_sums.1 = bf16[4,128,1024]{2,1,0:T(8,128)(2,1)} custom-call(bf16[128,4096]{1,0:T(8,128)(2,1)} %convolution_convert_fusion.refs_0_), custom_call_target="tpu_custom_call" | custom-call | tf_op jit(solution)/shard_map/dec_sums/pallas_call | solution.py:54
  175.7 1.5 convert_reduce_fusion.1
  177.2 1.7 add_convert_fusion
  (93 shorter events, 13.2 us)
Async XLA Ops:
  7.2 109.8 %copy-start = (bf16[384,512]{1,0:T(8,128)(2,1)S(1)}, bf16[384,512]{1,0:T(8,128)(2,1)}, u32[]{:S(2)}) copy-start(bf16[384,512]{1,0:T(8,128)(2,1)} %param.28) | copy-start | bytes 1179652
  7.2 83.0 %all-gather.3.cloned.1.call-start = ((), (), s32[]{:S(2)}) async-start(), calls=%async_computation | async-start | bytes 5898240 | tf_op jit(solution)/shard_map/all_gather | solution.py:191
  7.9 146.3 %all-gather.5.cloned.1.call-start = ((), (), s32[]{:S(2)}) async-start(), calls=%async_computation.1 | async-start | bytes 4718592 | tf_op jit(solution)/shard_map/all_gather | solution.py:192
  9.4 33.0 %collective-permute-start = (bf16[16,1536]{1,0:T(8,128)(2,1)}, bf16[16,1536]{1,0:T(8,128)(2,1)}, u32[]{:S(2)}, u32[]{:S(2)}) collective-permute-start(bf16[16,1536]{1,0:T(8,128)(2,1)} %get-tuple-element.41), channel_id=1, source_target_pairs={{0,1},{1,2},{2,3},{3,4},{4,5},{5,6},{6,7},{8,9},{9,10},{10,11},{11... | collective-permute-start | bytes 147464 | tf_op jit(solution)/shard_map/ppermute | solution.py:194
  12.4 30.0 %collective-permute-start.1 = (bf16[16,1536]{1,0:T(8,128)(2,1)}, bf16[16,1536]{1,0:T(8,128)(2,1)}, u32[]{:S(2)}, u32[]{:S(2)}) collective-permute-start(bf16[16,1536]{1,0:T(8,128)(2,1)} %get-tuple-element.42), channel_id=1, source_target_pairs={{1,0},{2,1},{3,2},{4,3},{5,4},{6,5},{7,6},{9,8},{10,9},{11,10},{12... | collective-permute-start | bytes 147464 | tf_op jit(solution)/shard_map/ppermute | solution.py:197
  13.7 2.6 %copy-start.6 = (bf16[1536,2,384]{2,1,0:T(2,128)(2,1)S(1)}, bf16[1536,2,384]{2,1,0:T(2,128)(2,1)}, u32[]{:S(2)}) copy-start(bf16[1536,2,384]{2,1,0:T(2,128)(2,1)} %param.18) | copy-start | bytes 7077892
  16.4 2.8 %copy-start.1 = (bf16[1024,1536]{1,0:T(8,128)(2,1)S(1)}, bf16[1024,1536]{1,0:T(8,128)(2,1)}, u32[]{:S(2)}) copy-start(bf16[1024,1536]{1,0:T(8,128)(2,1)} %param.16) | copy-start | bytes 9437188
  16.8 3.3 %copy-start.2 = (bf16[192,8,2,384]{3,1,2,0:T(8,128)(2,1)}, bf16[192,8,2,384]{3,1,2,0:T(8,128)(2,1)S(1)}, u32[]{:S(2)}) copy-start(bf16[192,8,2,384]{3,1,2,0:T(8,128)(2,1)S(1)} %copy.33) | copy-start | bytes 7077892
  19.1 1.0 copy-start.13
  22.9 1.3 copy-start.17
  22.9 1.9 %copy-start.12 = (s32[1024]{0:T(1024)S(1)}, s32[1024]{0:T(1024)}, u32[]{:S(2)}) copy-start(s32[1024]{0:T(1024)} %param.23) | copy-start | bytes 12292
  28.9 10.2 %copy-start.15 = (f32[1,384]{1,0:T(1,128)S(1)}, f32[1,384]{1,0:T(1,128)}, u32[]{:S(2)}) copy-start(f32[1,384]{1,0:T(1,128)} %broadcast_in_dim.44) | copy-start | bytes 4612
  32.9 11.7 %copy-start.14 = (f32[1536]{0:T(1024)S(1)}, f32[1536]{0:T(1024)}, u32[]{:S(2)}) copy-start(f32[1536]{0:T(1024)} %param.17) | copy-start | bytes 18436
  42.4 4.5 %copy-start.5 = (bf16[1024,384]{1,0:T(8,128)(2,1)S(1)}, bf16[1024,384]{1,0:T(8,128)(2,1)}, u32[]{:S(2)}) copy-start(bf16[1024,384]{1,0:T(8,128)(2,1)} %fusion.55) | copy-start | bytes 2359300
  78.6 1.4 copy-start.10
  88.6 1.2 copy-start.3
  95.7 15.1 %copy-start.16 = (s32[1024]{0:T(1024)S(1)}, s32[1024]{0:T(1024)}, u32[]{:S(2)}) copy-start(s32[1024]{0:T(1024)} %get-tuple-element.46) | copy-start | bytes 12292
  95.7 15.1 %copy-start.19 = (f32[1024]{0:T(1024)S(1)}, f32[1024]{0:T(1024)}, u32[]{:S(2)}) copy-start(f32[1024]{0:T(1024)} %param.22) | copy-start | bytes 12292
  110.8 6.5 %copy-start.9 = (bf16[384,512]{1,0:T(8,128)(2,1)S(1)}, bf16[384,512]{1,0:T(8,128)(2,1)}, u32[]{:S(2)}) copy-start(bf16[384,512]{1,0:T(8,128)(2,1)} %param.29) | copy-start | bytes 1179652
  113.4 3.4 %collective-permute-start.2 = (f32[1,384]{1,0:T(1,128)S(1)}, f32[1,384]{1,0:T(1,128)S(1)}, u32[]{:S(2)}, u32[]{:S(2)}) collective-permute-start(f32[1,384]{1,0:T(1,128)S(1)} %constant_dynamic-slice_fusion), channel_id=1, source_target_pairs={{0,1},{1,2},{2,3},{3,4},{4,5},{5,6},{6,7},{8,9},{9,10},{10,11},{11... | collective-permute-start | bytes 4616 | tf_op jit(solution)/shard_map/ppermute | solution.py:251
  116.9 13.3 %copy-start.7 = (bf16[256,384]{1,0:T(8,128)(2,1)}, bf16[256,384]{1,0:T(8,128)(2,1)S(1)}, u32[]{:S(2)}) copy-start(bf16[256,384]{1,0:T(8,128)(2,1)S(1)} %select_convert_fusion) | copy-start | bytes 589828
  117.5 14.0 %copy-start.18 = (f32[128]{0:T(128)S(1)}, f32[128]{0:T(128)}, u32[]{:S(2)}) copy-start(f32[128]{0:T(128)} %param.30) | copy-start | bytes 1540
  130.2 20.8 %copy-start.11 = (bf16[128,4,128]{2,0,1:T(8,128)(2,1)S(1)}, bf16[128,4,128]{2,0,1:T(8,128)(2,1)}, u32[]{:S(2)}) copy-start(bf16[128,4,128]{2,0,1:T(8,128)(2,1)} %fusion.77) | copy-start | bytes 393220
  151.0 2.3 %copy-start.8 = (bf16[2176,256]{1,0:T(8,128)(2,1)S(1)}, bf16[2176,256]{1,0:T(8,128)(2,1)}, u32[]{:S(2)}) copy-start(bf16[2176,256]{1,0:T(8,128)(2,1)} %kv_rows.1) | copy-start | bytes 3342340
  175.6 3.3 %copy-start.4 = (bf16[1024,384]{1,0:T(8,128)(2,1)S(1)}, bf16[1024,384]{1,0:T(8,128)(2,1)}, u32[]{:S(2)}) copy-start(bf16[1024,384]{1,0:T(8,128)(2,1)} %to_channels.1) | copy-start | bytes 2359300
Sparse Core Ops, SparseCore 0:
  9.8 71.2 all-gather.2
  82.7 46.8 all-gather.4

commit v2 on v1

--- a/solution.py
+++ b/solution.py
@@ -15,18 +15,37 @@
 MESH = pl.DeviceIdType.MESH
 
 
-def exchange_kernel(axis, n, routes, *refs):
+def exchange_kernel(axis, n, routes, swap, *refs):
     m = len(routes)
-    xs, outs = refs[:m], refs[m : 2 * m]
-    send, recv, own = refs[2 * m :]
+    e = m + (swap is not None)
+    xs, outs = refs[:e], refs[e : 2 * e]
+    send, recv, own = refs[2 * e :]
     me = lax.axis_index(axis)
     barrier = pltpu.get_barrier_semaphore()
+    if swap is not None:
+        core = lax.rem(lax.axis_index(swap), 2)
+        mate = lax.axis_index(swap) + 1 - 2 * core
+        pl.semaphore_signal(barrier, inc=1, device_id={swap: mate}, device_id_type=MESH)
     for k in range(1, n):
         pl.semaphore_signal(
             barrier, inc=1, device_id={axis: lax.rem(me + k, n)}, device_id_type=MESH
         )
-    pl.semaphore_wait(barrier, n - 1)
+    pl.semaphore_wait(barrier, n - 1 + (swap is not None))
     copies = []
+    if swap is not None:
+        copy = pltpu.make_async_remote_copy(
+            src_ref=xs[m],
+            dst_ref=outs[m].at[:, core],
+            send_sem=send.at[m, 0],
+            recv_sem=recv.at[m, 0],
+            device_id={swap: mate},
+            device_id_type=MESH,
+        )
+        copy.start()
+        copies.append(copy)
+        mine = pltpu.make_async_copy(xs[m], outs[m].at[:, core], own.at[m])
+        mine.start()
+        copies.append(mine)
     for i, (take, put) in enumerate(routes):
         for k in range(1, n):
             peer = lax.rem(me + k, n)
@@ -47,12 +66,12 @@
         copy.wait()
 
 
-def exchange(arrays, shapes, routes, axis, collective_id, name):
+def exchange(arrays, shapes, routes, axis, collective_id, name, swap=None):
     n = lax.axis_size(axis)
     m = len(arrays)
     vmem = pl.BlockSpec(memory_space=pltpu.VMEM)
     return pl.pallas_call(
-        functools.partial(exchange_kernel, axis, n, routes),
+        functools.partial(exchange_kernel, axis, n, routes, swap),
         out_shape=[jax.ShapeDtypeStruct(s, a.dtype) for s, a in zip(shapes, arrays)],
         in_specs=[vmem] * m,
         out_specs=[vmem] * m,
@@ -188,7 +207,17 @@
     tap_total = channelwise_filter_taps.shape[0]
     f32, bf16 = jnp.float32, jnp.bfloat16
 
-    exit_all = lax.all_gather(unitwise_exit_coefficients, "grp", axis=0, tiled=True)
+    half_rows = unitwise_exit_coefficients.shape[0] // 2
+    exit_half = lax.all_gather(
+        lax.dynamic_slice_in_dim(
+            unitwise_exit_coefficients,
+            lax.rem(lax.axis_index("seq"), 2) * half_rows,
+            half_rows,
+            0,
+        ),
+        "grp",
+        axis=0,
+    )
     mixing_all = lax.all_gather(mixing_exit_coefficients, "seq", axis=1, tiled=True)
 
     before = lax.ppermute(
@@ -210,14 +239,20 @@
         [channelwise_filter_taps, filtering_rescale_factors[None, :]], axis=0
     )
     strip = share + 2 * RIM
-    strips, taps_all = exchange(
-        [widened, packed_taps],
-        [(strip, feature_width), (tap_total + 1, feature_width)],
+    strips, taps_all, exit_all = exchange(
+        [widened, packed_taps, exit_half],
+        [
+            (strip, feature_width),
+            (tap_total + 1, feature_width),
+            (groups, 2, half_rows, feature_width),
+        ],
         [(rows_at(share, strip), cols_at(columns)), (whole, cols_at(columns))],
         "grp",
         1,
         "to_frames",
-    )
+        swap="seq",
+    )
+    exit_all = exit_all.reshape(feature_width, feature_width)
 
     strips_f = strips.astype(f32)
     shift = RIM - tap_total // 2

time: 188 us -> 175 us (0.931)
  Pallas kernels: 92.7 us -> 81.2 us
  matrix products: 24.7 us -> 21.9 us
    pallas_call x4, Pallas kernels: 75 us -> 64.3 us  [exchange(): pl.pallas_call(functools.partial(exchange_kernel, axis, n, routes, swap),...]
    all_gather x1, waiting for transfers between devices: 0.02 us -> 2.49 us  [local(): lax.all_gather(lax.dynamic_slice_in_dim(unitwise_exit_coefficients, lax.r...]
    dot_general x1, matrix products: 5.54 us -> 3.66 us  [local(): jnp.dot(activated, exit_all, preferred_element_type=f32)]
    unnamed x43 -> x45, local copies, waits for them, and re-layouts: 5.08 us -> 4.41 us
  transfers between devices with their start and end apart: 5 -> 5, of which waited for: 0 -> 1; matrix products, arithmetic and copies ran while one was open for 31% -> 32% of each run, Pallas kernels for 40% -> 36%
where the time goes in v2:
time: 175 us; the launch traced here: 174 us
  Pallas kernels  81.2 us (46%)
  other arithmetic  33.5 us (19%)
  matrix products  21.9 us (13%)
  between operations  16.9 us (10%)
  local copies, waits for them, and re-layouts  11.7 us (7%)
  starting transfers between devices  6 us (3%)
  waiting for transfers between devices  2.55 us (1%)
    pallas_call x4, Pallas kernels, exchange(): pl.pallas_call(functools.partial(exchange_kernel, axis, n, routes, swap),...  64.3 us
    pallas_call x1, Pallas kernels, gather_pairs(): pl.pallas_call(functools.partial(gather_pairs_kernel, axis, n), out_shape...  16.8 us
    reduce_sum x3, other arithmetic, layer_norm(): center = jnp.mean(inputs, axis=-1, keepdims=True)  11.6 us
    unnamed x45, local copies, waits for them, and re-layouts  4.41 us
    dot_general x2, matrix products, gate(): projected = jnp.dot(normed, entry, preferred_element_type=f32)  4.17 us
    dot_general x1, matrix products, local(): jnp.dot(dec_normed, probe_projection_coefficients, preferred_element_type...  4 us
    dot_general x1, matrix products, local(): jnp.dot(attended, mixing_all, preferred_element_type=f32).astype(bf16)  3.93 us
    dot_general x1, matrix products, local(): jnp.dot(activated, exit_all, preferred_element_type=f32)  3.66 us
  transfers between devices with their start and end apart: 5, of which 1 were waited for; matrix products, arithmetic and copies ran while one was open for 32% of the time, Pallas kernels for 36%

profile of v2, /device:TPU:0, one launch (start us, length us, event | category | flops | bytes accessed | tf_op | source)
XLA Modules:
  0.0 173.6 jit_solution(10182188719069970802)
XLA Ops:
  7.2 1.2 copy-done
  9.4 1.5 fusion.98
  10.8 3.0 %collective-permute-start = (bf16[16,1536]{1,0:T(8,128)(2,1)}, bf16[16,1536]{1,0:T(8,128)(2,1)}, u32[]{:S(2)}, u32[]{:S(2)}) collective-permute-start(bf16[16,1536]{1,0:T(8,128)(2,1)} %get-tuple-element.43), channel_id=1, source_target_pairs={{0,1},{1,2},{2,3},{3,4},{4,5},{5,6},{6,7},{8,9},{9,10},{10,11},{11... | collective-permute-start | bytes 147464 | tf_op jit(solution)/shard_map/ppermute | solution.py:223
  13.8 1.3 collective-permute-start.1
  15.2 2.5 %convert_reduce_fusion = f32[1024]{0:T(1024)S(1)} fusion(bf16[1024,1536]{1,0:T(8,128)(2,1)} %param.16), kind=kLoop, calls=%fused_computation.1 | loop fusion | flops 3144704 | bytes 3149824 | tf_op jit(solution)/shard_map/reduce_sum | solution.py:172
  18.3 1.6 copy-done.1
  20.8 2.8 %fusion.7 = f32[1024,768]{1,0:T(8,128)S(1)} fusion(bf16[1536,768]{1,0:T(8,128)(2,1)S(1)} %bitcast.51, bf16[1024,1536]{1,0:T(8,128)(2,1)S(1)} %copy-done.1, f32[1536]{0:T(1024)S(1)} %copy-done.12, f32[1024]{0:T(1024)S(1)} %add_rsqrt_fusion, f32[1024]{0:T(1024)S(1)} %broadcast_multiply_fusion), kind=kOutput, calls=%fused_computation.11 | convolution fusion | flops 2423783424 | bytes 8665088 | tf_op jit(solution)/shard_map/dot_general | solution.py:233
  23.6 1.3 fusion.55
  26.0 2.0 %fusion.100 = (s32[]{:T(128)}, s32[1024]{0:T(1024)}) fusion(s32[1024]{0:T(1024)} %param.23, s32[8,128]{1,0:T(8,128)S(1)} %reduce-window.9, s32[8]{0:T(128)S(1)} %slice_reduce_fusion.32), kind=kLoop, calls=%fused_computation.203 | loop fusion | flops 3071 | bytes 12324 | tf_op jit(solution)/shard_map/reduce_sum | solution.py:280
  28.0 1.5 fusion.15
  29.5 4.0 %fusion.64 = f32[128,512]{1,0:T(8,128)} fusion(bf16[4096,512]{1,0:T(8,128)(2,1)} %param.26, bf16[128,4096]{1,0:T(8,128)(2,1)} %param.24, f32[4096]{0:T(1024)} %param.25, f32[128]{0:T(128)S(1)} %add_rsqrt_fusion.4), kind=kOutput, calls=%fused_computation.103 | convolution fusion | flops 538968064 | bytes 5521920 | tf_op jit(solution)/shard_map/dot_general | solution.py:333
  33.5 1.7 %reshape.145 = f32[128,4,128]{2,1,0:T(4,128)} reshape(f32[128,512]{1,0:T(8,128)} %fusion.64) | data formatting | bytes 524288 | tf_op jit(solution)/shard_map/reshape | solution.py:335
  35.3 1.8 %multiply_reduce_fusion.1 = f32[128,4]{1,0:T(8,128)} fusion(f32[128,4,128]{2,1,0:T(4,128)} %reshape.145), kind=kLoop, calls=%fused_computation.123 | loop fusion | flops 130560 | bytes 264192 | tf_op jit(solution)/shard_map/reduce_sum | solution.py:178
  38.0 1.8 %fusion.77 = bf16[128,4,128]{2,0,1:T(8,128)(2,1)} fusion(f32[128]{0:T(128)} %param.27, f32[128,4]{0,1:T(4,128)S(1)} %add_rsqrt_fusion.1, f32[128,512]{1,0:T(8,128)} %fusion.64), kind=kLoop, calls=%fused_computation.122 | loop fusion | flops 196608 | bytes 395776 | tf_op jit(solution)/shard_map/convert_element_type | solution.py:336
  39.8 1.4 pad_maximum_fusion.4.refs_1_
  45.0 1.4 fusion.83
  47.4 2.5 %all-gather.6.cloned.1.call-done = bf16[768,1536]{1,0:T(8,128)(2,1)} async-done(((bf16[192,1536]{1,0:T(8,128)(2,1)}), bf16[768,1536]{1,0:T(8,128)(2,1)}) %all-gather.6.cloned.1.call-update) | async-done | bytes 2359312 | tf_op jit(solution)/shard_map/all_gather | solution.py:211
  49.9 20.5 %to_frames.1 = (bf16[288,1536]{1,0:T(8,128)(2,1)}, f32[32,1536]{1,0:T(8,128)}, bf16[4,2,192,1536]{3,2,1,0:T(8,128)(2,1)}) custom-call(bf16[1056,384]{1,0:T(8,128)(2,1)} %pad_maximum_fusion.refs_0_, f32[32,384]{1,0:T(8,128)} %pad_maximum_fusion.4.refs_1_, bf16[4,192,1536]{2,1,0:T(8,128)(2,1)} %bitcast.54), custom_call_target="tpu_custom_call" | custom-call | tf_op jit(solution)/shard_map/to_frames/pallas_call | solution.py:73
  70.5 1.4 convert_element_type.100
  72.5 8.1 %fusion.96 = (f32[256]{0:T(256)S(1)}, f32[256,1536]{1,0:T(8,128)S(1)}) fusion(f32[288,1536]{1,0:T(8,128)S(1)} %convert_element_type.100, f32[1536]{0:T(1024)S(1)} %get-tuple-element.10, f32[1536]{0:T(1024)S(1)} %get-tuple-element.11, f32[1536]{0:T(1024)S(1)} %get-tuple-element.12, f32[1536]{0:T(1024)S(1)} %get-tuple-element.13, ...), kind=kLoop, calls=%fused_computation.200 | loop fusion | flops 24379136 | bytes 50523136 | tf_op jit(solution)/shard_map/reduce_sum | solution.py:172
  80.9 3.7 %fusion.12.refs_0_ = bf16[256,1536]{1,0:T(8,128)(2,1)} fusion(bf16[1536,1536]{1,0:T(8,128)(2,1)S(1)} %bitcast.62, f32[256,1536]{1,0:T(8,128)S(1)} %get-tuple-element.42, f32[1536]{0:T(1024)S(1)} %get-tuple-element.9, f32[256]{0:T(256)S(1)} %add_rsqrt_fusion.3, f32[256]{0:T(256)S(1)} %broadcast_multiply_fusion.1, bf16[1024,1536]{1,0:T(8,128)(2,1)} %param.16, ...), kind=kOutput, calls=%fused_computation.18 | convolution fusion | flops 1212284928 | bytes 7872516 | tf_op jit(solution)/shard_map/dot_general | solution.py:268
  84.6 13.9 %to_channels.1 = bf16[1024,384]{1,0:T(8,128)(2,1)} custom-call(bf16[256,1536]{1,0:T(8,128)(2,1)} %fusion.12.refs_0_), custom_call_target="tpu_custom_call" | custom-call | tf_op jit(solution)/shard_map/to_channels/pallas_call | solution.py:73
  98.5 2.5 %fusion.52 = f32[256,384]{1,0:T(8,128)S(1)} fusion(bf16[1024,384]{1,0:T(8,128)(2,1)} %to_channels.1, f32[1024]{0:T(1024)S(1)} %copy-done.18, s32[1024]{0:T(1024)S(1)} %copy-done.15), kind=kOutput, calls=%fused_computation.91 | convolution fusion | flops 1209008128 | bytes 1187840 | tf_op jit(solution)/shard_map/dot_general | solution.py:284
  101.1 1.6 collective-permute-start.2
  105.6 12.0 %kv_heads.1 = bf16[4,2,256,128]{3,2,1,0:T(8,128)(2,1)} custom-call(bf16[2,256,512]{2,1,0:T(8,128)(2,1)} %pad_maximum_fusion.1.refs_0_), custom_call_target="tpu_custom_call" | custom-call | tf_op jit(solution)/shard_map/kv_heads/pallas_call | solution.py:73
  117.6 1.2 convert_reduce_fusion.2
  119.7 16.8 %kv_rows.1 = bf16[2176,256]{1,0:T(8,128)(2,1)} custom-call(bf16[272,256]{1,0:T(8,128)(2,1)} %pad_maximum_fusion.2.x_ref), custom_call_target="tpu_custom_call" | custom-call | tf_op jit(solution)/shard_map/kv_rows/pallas_call | solution.py:158
  137.6 2.3 %fusion.101 = (f32[512]{0:T(512)S(1)}, bf16[512,2176]{1,0:T(8,128)(2,1)S(1)}) fusion(bf16[512,128]{1,0:T(8,128)(2,1)S(1)} %bitcast.57, bf16[2176,256]{1,0:T(8,128)(2,1)} %kv_rows.1, pred[2176]{0:T(1024)(128)(4,1)S(1)} %lt.52), kind=kOutput, calls=%fused_computation.204 | convolution fusion | flops 289668608 | bytes 2920576 | tf_op jit(solution)/shard_map/dot_general | solution.py:340
  140.8 3.9 %convolution_convert_fusion.refs_0_ = bf16[128,4096]{1,0:T(8,128)(2,1)} fusion(bf16[128,512]{0,1:T(8,128)(2,1)S(1)} %bitcast.56, bf16[512,4096]{1,0:T(8,128)(2,1)} %all-gather.4.cloned.1.call-done), kind=kOutput, calls=%fused_computation.10 | convolution fusion | flops 537395200 | bytes 5373952 | tf_op jit(solution)/shard_map/dot_general | solution.py:357
  144.8 17.9 %dec_sums.1 = bf16[4,128,1024]{2,1,0:T(8,128)(2,1)} custom-call(bf16[128,4096]{1,0:T(8,128)(2,1)} %convolution_convert_fusion.refs_0_), custom_call_target="tpu_custom_call" | custom-call | tf_op jit(solution)/shard_map/dec_sums/pallas_call | solution.py:73
  162.6 1.5 convert_reduce_fusion.1
  164.2 1.7 add_convert_fusion
  (97 shorter events, 14.4 us)
Async XLA Ops:
  7.2 1.3 copy-start
  7.2 42.7 %all-gather.6.cloned.1.call-start = ((), (), s32[]{:S(2)}) async-start(), calls=%async_computation.1 | async-start | bytes 2949120 | tf_op jit(solution)/shard_map/all_gather | solution.py:211
  9.3 131.5 %all-gather.4.cloned.1.call-start = ((), (), s32[]{:S(2)}) async-start(), calls=%async_computation | async-start | bytes 4718592 | tf_op jit(solution)/shard_map/all_gather | solution.py:221
  10.8 32.1 %collective-permute-start = (bf16[16,1536]{1,0:T(8,128)(2,1)}, bf16[16,1536]{1,0:T(8,128)(2,1)}, u32[]{:S(2)}, u32[]{:S(2)}) collective-permute-start(bf16[16,1536]{1,0:T(8,128)(2,1)} %get-tuple-element.43), channel_id=1, source_target_pairs={{0,1},{1,2},{2,3},{3,4},{4,5},{5,6},{6,7},{8,9},{9,10},{10,11},{11... | collective-permute-start | bytes 147464 | tf_op jit(solution)/shard_map/ppermute | solution.py:223
  13.8 29.1 %collective-permute-start.1 = (bf16[16,1536]{1,0:T(8,128)(2,1)}, bf16[16,1536]{1,0:T(8,128)(2,1)}, u32[]{:S(2)}, u32[]{:S(2)}) collective-permute-start(bf16[16,1536]{1,0:T(8,128)(2,1)} %get-tuple-element.44), channel_id=1, source_target_pairs={{1,0},{2,1},{3,2},{4,3},{5,4},{6,5},{7,6},{9,8},{10,9},{11,10},{12... | collective-permute-start | bytes 147464 | tf_op jit(solution)/shard_map/ppermute | solution.py:226
  15.1 2.6 %copy-start.4 = (bf16[1536,2,384]{2,1,0:T(2,128)(2,1)S(1)}, bf16[1536,2,384]{2,1,0:T(2,128)(2,1)}, u32[]{:S(2)}) copy-start(bf16[1536,2,384]{2,1,0:T(2,128)(2,1)} %param.18) | copy-start | bytes 7077892
  17.8 2.1 %copy-start.1 = (bf16[1024,1536]{1,0:T(8,128)(2,1)S(1)}, bf16[1024,1536]{1,0:T(8,128)(2,1)}, u32[]{:S(2)}) copy-start(bf16[1024,1536]{1,0:T(8,128)(2,1)} %param.16) | copy-start | bytes 9437188
  19.8 1.0 copy-start.12
  23.6 1.3 copy-start.16
  23.6 1.9 %copy-start.11 = (s32[1024]{0:T(1024)S(1)}, s32[1024]{0:T(1024)}, u32[]{:S(2)}) copy-start(s32[1024]{0:T(1024)} %param.23) | copy-start | bytes 12292
  29.5 10.2 %copy-start.14 = (f32[1,384]{1,0:T(1,128)S(1)}, f32[1,384]{1,0:T(1,128)}, u32[]{:S(2)}) copy-start(f32[1,384]{1,0:T(1,128)} %broadcast_in_dim.44) | copy-start | bytes 4612
  33.5 11.5 %copy-start.13 = (f32[1536]{0:T(1024)S(1)}, f32[1536]{0:T(1024)}, u32[]{:S(2)}) copy-start(f32[1536]{0:T(1024)} %param.17) | copy-start | bytes 18436
  42.9 3.5 %copy-start.3 = (bf16[1024,384]{1,0:T(8,128)(2,1)S(1)}, bf16[1024,384]{1,0:T(8,128)(2,1)}, u32[]{:S(2)}) copy-start(bf16[1024,384]{1,0:T(8,128)(2,1)} %fusion.55) | copy-start | bytes 2359300
  70.5 1.4 copy-start.9
  72.5 8.4 %slice-start = ((s8[4718592]{0:T(1024)(128)(4,1)}), s8[4194304]{0:T(1024)(128)(4,1)S(1)}, s32[]{:S(2)}) async-start(s8[4718592]{0:T(1024)(128)(4,1)} %bitcast.60), calls=%async_computation.2 | async-start | bytes 8388608
  72.5 8.4 %slice-start.1 = ((s8[4718592]{0:T(1024)(128)(4,1)}), s8[524288]{0:T(1024)(128)(4,1)S(1)}, s32[]{:S(2)}) async-start(s8[4718592]{0:T(1024)(128)(4,1)} %bitcast.60), calls=%async_computation.3 | async-start | bytes 1048576
  84.6 13.9 %copy-start.15 = (s32[1024]{0:T(1024)S(1)}, s32[1024]{0:T(1024)}, u32[]{:S(2)}) copy-start(s32[1024]{0:T(1024)} %get-tuple-element.48) | copy-start | bytes 12292
  84.6 13.9 %copy-start.18 = (f32[1024]{0:T(1024)S(1)}, f32[1024]{0:T(1024)}, u32[]{:S(2)}) copy-start(f32[1024]{0:T(1024)} %param.22) | copy-start | bytes 12292
  84.6 19.5 %copy-start.7 = (bf16[384,512]{1,0:T(8,128)(2,1)S(1)}, bf16[384,512]{1,0:T(8,128)(2,1)}, u32[]{:S(2)}) copy-start(bf16[384,512]{1,0:T(8,128)(2,1)} %param.28) | copy-start | bytes 1179652
  98.5 5.9 %copy-start.8 = (bf16[384,512]{1,0:T(8,128)(2,1)S(1)}, bf16[384,512]{1,0:T(8,128)(2,1)}, u32[]{:S(2)}) copy-start(bf16[384,512]{1,0:T(8,128)(2,1)} %param.29) | copy-start | bytes 1179652
  101.1 2.8 %collective-permute-start.2 = (f32[1,384]{1,0:T(1,128)S(1)}, f32[1,384]{1,0:T(1,128)S(1)}, u32[]{:S(2)}, u32[]{:S(2)}) collective-permute-start(f32[1,384]{1,0:T(1,128)S(1)} %constant_dynamic-slice_fusion), channel_id=1, source_target_pairs={{0,1},{1,2},{2,3},{3,4},{4,5},{5,6},{6,7},{8,9},{9,10},{10,11},{11... | collective-permute-start | bytes 4616 | tf_op jit(solution)/shard_map/ppermute | solution.py:286
  104.1 13.5 %copy-start.5 = (bf16[256,384]{1,0:T(8,128)(2,1)}, bf16[256,384]{1,0:T(8,128)(2,1)S(1)}, u32[]{:S(2)}) copy-start(bf16[256,384]{1,0:T(8,128)(2,1)S(1)} %select_convert_fusion) | copy-start | bytes 589828
  104.7 14.2 %copy-start.17 = (f32[128]{0:T(128)S(1)}, f32[128]{0:T(128)}, u32[]{:S(2)}) copy-start(f32[128]{0:T(128)} %param.30) | copy-start | bytes 1540
  117.6 20.0 %copy-start.10 = (bf16[128,4,128]{2,0,1:T(8,128)(2,1)S(1)}, bf16[128,4,128]{2,0,1:T(8,128)(2,1)}, u32[]{:S(2)}) copy-start(bf16[128,4,128]{2,0,1:T(8,128)(2,1)} %fusion.77) | copy-start | bytes 393220
  137.6 2.3 %copy-start.6 = (bf16[2176,256]{1,0:T(8,128)(2,1)S(1)}, bf16[2176,256]{1,0:T(8,128)(2,1)}, u32[]{:S(2)}) copy-start(bf16[2176,256]{1,0:T(8,128)(2,1)} %kv_rows.1) | copy-start | bytes 3342340
  162.6 3.3 %copy-start.2 = (bf16[1024,384]{1,0:T(8,128)(2,1)S(1)}, bf16[1024,384]{1,0:T(8,128)(2,1)}, u32[]{:S(2)}) copy-start(bf16[1024,384]{1,0:T(8,128)(2,1)} %to_channels.1) | copy-start | bytes 2359300
Sparse Core Ops, SparseCore 0:
  9.8 40.0 all-gather.5
  51.5 46.8 all-gather.3

commit v3 on v1

--- a/solution.py
+++ b/solution.py
@@ -15,10 +15,11 @@
 MESH = pl.DeviceIdType.MESH
 
 
-def exchange_kernel(axis, n, routes, *refs):
+def exchange_kernel(axis, n, routes, extra, *refs):
     m = len(routes)
-    xs, outs = refs[:m], refs[m : 2 * m]
-    send, recv, own = refs[2 * m :]
+    e_in, e_out = (extra[0], extra[1]) if extra else (0, 0)
+    xs, outs = refs[:m], refs[m + e_in : 2 * m + e_in]
+    send, recv, own = refs[2 * m + e_in + e_out :]
     me = lax.axis_index(axis)
     barrier = pltpu.get_barrier_semaphore()
     for k in range(1, n):
@@ -43,19 +44,76 @@
         mine = pltpu.make_async_copy(take(xs[i], me), put(outs[i], me), own.at[i])
         mine.start()
         copies.append(mine)
+    if extra:
+        extra[2](*refs[m : m + e_in], *refs[2 * m + e_in : 2 * m + e_in + e_out])
     for copy in copies:
         copy.wait()
 
 
-def exchange(arrays, shapes, routes, axis, collective_id, name):
+def query_body(text_ref, scale_ref, probe_ref, gain_ref, out_ref):
+    rows, width = text_ref.shape
+    head_dim = gain_ref.shape[1]
+    step = 512
+    squares = jnp.zeros((rows, 1), jnp.float32)
+    for c in range(0, width, step):
+        x = text_ref[:, c : c + step].astype(jnp.float32)
+        squares = squares + jnp.sum(x * x, axis=-1, keepdims=True)
+    factor = lax.rsqrt(squares / width + EPS_ROOT)
+    total = jnp.zeros((rows, probe_ref.shape[1]), jnp.float32)
+    for c in range(0, width, step):
+        x = text_ref[:, c : c + step].astype(jnp.float32)
+        x = (x * factor * scale_ref[:, c : c + step]).astype(jnp.bfloat16)
+        total = total + jnp.dot(x, probe_ref[c : c + step, :], preferred_element_type=jnp.float32)
+    for h in range(total.shape[1] // head_dim):
+        part = total[:, h * head_dim : (h + 1) * head_dim]
+        part = part * lax.rsqrt(jnp.mean(part * part, axis=-1, keepdims=True) + EPS_ROOT)
+        out_ref[h * rows : (h + 1) * rows, :] = (part * gain_ref[...]).astype(jnp.bfloat16)
+
+
+def swap_kernel(axis, x_ref, o_ref, send, recv, own):
+    core = lax.rem(lax.axis_index(axis), 2)
+    mate = lax.axis_index(axis) + 1 - 2 * core
+    barrier = pltpu.get_barrier_semaphore()
+    pl.semaphore_signal(barrier, inc=1, device_id={axis: mate}, device_id_type=MESH)
+    pl.semaphore_wait(barrier, 1)
+    copy = pltpu.make_async_remote_copy(
+        src_ref=x_ref, dst_ref=o_ref.at[:, core], send_sem=send, recv_sem=recv,
+        device_id={axis: mate}, device_id_type=MESH,
+    )
+    copy.start()
+    mine = pltpu.make_async_copy(x_ref, o_ref.at[:, core], own)
+    mine.start()
+    copy.wait()
+    mine.wait()
+
+
+def swap_halves(x, axis, collective_id, name):
+    vmem = pl.BlockSpec(memory_space=pltpu.VMEM)
+    dma = pltpu.SemaphoreType.DMA
+    return pl.pallas_call(
+        functools.partial(swap_kernel, axis),
+        out_shape=jax.ShapeDtypeStruct((x.shape[0], 2) + x.shape[1:], x.dtype),
+        in_specs=[vmem],
+        out_specs=vmem,
+        scratch_shapes=[dma(()), dma(()), dma(())],
+        compiler_params=pltpu.CompilerParams(
+            collective_id=collective_id, has_side_effects=True
+        ),
+        name=name,
+    )(x)
+
+
+def exchange(arrays, shapes, routes, axis, collective_id, name, operands=(), results=(), body=None):
     n = lax.axis_size(axis)
     m = len(arrays)
     vmem = pl.BlockSpec(memory_space=pltpu.VMEM)
+    extra = (len(operands), len(results), body) if body else None
     return pl.pallas_call(
-        functools.partial(exchange_kernel, axis, n, routes),
-        out_shape=[jax.ShapeDtypeStruct(s, a.dtype) for s, a in zip(shapes, arrays)],
-        in_specs=[vmem] * m,
-        out_specs=[vmem] * m,
+        functools.partial(exchange_kernel, axis, n, routes, extra),
+        out_shape=[jax.ShapeDtypeStruct(s, a.dtype) for s, a in zip(shapes, arrays)]
+        + list(results),
+        in_specs=[vmem] * (m + len(operands)),
+        out_specs=[vmem] * (m + len(results)),
         scratch_shapes=[
             pltpu.SemaphoreType.DMA((m, n)),
             pltpu.SemaphoreType.DMA((m, n)),
@@ -65,7 +123,7 @@
             collective_id=collective_id, has_side_effects=True
         ),
         name=name,
-    )(*arrays)
+    )(*arrays, *operands)
 
 
 def rows_at(size, length=None):
@@ -87,20 +145,13 @@
 
 def gather_pairs_kernel(axis, n, x_ref, o_ref, send, recv, mate_send, mate_recv, own):
     rows = x_ref.shape[0]
-    half = n // 2
+    chips = n // 2
     me = lax.axis_index(axis)
+    chip = me // 2
     mate = me + 1 - 2 * lax.rem(me, 2)
 
     def place(i):
         return o_ref.at[pl.ds(pl.multiple_of(i * rows, rows), rows), :]
-
-    barrier = pltpu.get_barrier_semaphore()
-    for k in range(1, half):
-        pl.semaphore_signal(
-            barrier, inc=1, device_id={axis: lax.rem(me + 2 * k, n)}, device_id_type=MESH
-        )
-    pl.semaphore_signal(barrier, inc=1, device_id={axis: mate}, device_id_type=MESH)
-    pl.semaphore_wait(barrier, half)
 
     def over(src, dst, s, r, device):
         return pltpu.make_async_remote_copy(
@@ -108,40 +159,93 @@
             device_id={axis: device}, device_id_type=MESH,
         )
 
-    copies, forwards = [], []
-    for k in range(1, half):
-        copy = over(x_ref, place(me), send.at[k], recv.at[k], lax.rem(me + 2 * k, n))
-        copy.start()
-        copies.append(copy)
-    first = over(x_ref, place(me), mate_send.at[0], mate_recv.at[0], mate)
+    up, down = lax.rem(me + 2, n), lax.rem(me + n - 2, n)
+    has_up, has_down = chip < chips - 1, chip > 0
+    barrier = pltpu.get_barrier_semaphore()
+    pl.semaphore_signal(barrier, inc=1, device_id={axis: mate}, device_id_type=MESH)
+
+    @pl.when(has_up)
+    def _():
+        pl.semaphore_signal(barrier, inc=1, device_id={axis: up}, device_id_type=MESH)
+
+    @pl.when(has_down)
+    def _():
+        pl.semaphore_signal(barrier, inc=1, device_id={axis: down}, device_id_type=MESH)
+
+    pl.semaphore_wait(barrier, 1 + has_up.astype(jnp.int32) + has_down.astype(jnp.int32))
+
+    def hop(side, step, src):
+        origin = me - 2 * step if side == 0 else me + 2 * step
+        origin = lax.rem(origin + n, n)
+        target = up if side == 0 else down
+        source = src if src is not None else place(origin)
+        return over(source, place(origin), send.at[side, step], recv.at[side, step], target)
+
+    def sends(side, step):
+        if side == 0:
+            return jnp.logical_and(has_up, chip >= step)
+        return jnp.logical_and(has_down, chip + step < chips)
+
+    def arrives(side, step):
+        return chip >= step + 1 if side == 0 else chip + step + 1 < chips
+
+    def hand_on(side, step):
+        origin = me - 2 * (step + 1) if side == 0 else me + 2 * (step + 1)
+        spot = place(lax.rem(origin + n, n))
+        return over(spot, spot, mate_send.at[side, step], mate_recv.at[side, step], mate)
+
+    for side in range(2):
+
+        @pl.when(sends(side, 0))
+        def _(side=side):
+            hop(side, 0, x_ref).start()
+
+    first = over(x_ref, place(me), own.at[0], own.at[1], mate)
     first.start()
-    forwards.append(first)
-    mine = pltpu.make_async_copy(x_ref, place(me), own)
+    mine = pltpu.make_async_copy(x_ref, place(me), own.at[2])
     mine.start()
-    for k in range(1, half):
-        copies[k - 1].wait_recv()
-        origin = lax.rem(me + n - 2 * k, n)
-        hand = over(place(origin), place(origin), mate_send.at[k], mate_recv.at[k], mate)
-        hand.start()
-        forwards.append(hand)
-    for hand in forwards:
-        hand.wait()
-    for copy in copies:
-        copy.wait_send()
+    for step in range(chips - 1):
+        for side in range(2):
+
+            @pl.when(arrives(side, step))
+            def _(side=side, step=step):
+                hop(side, step, x_ref).wait_recv()
+
+            if step + 1 < chips - 1:
+
+                @pl.when(sends(side, step + 1))
+                def _(side=side, step=step):
+                    hop(side, step + 1, None).start()
+
+            @pl.when(arrives(side, step))
+            def _(side=side, step=step):
+                hand_on(side, step).start()
+
+    first.wait()
     mine.wait()
+    for step in range(chips - 1):
+        for side in range(2):
+
+            @pl.when(arrives(side, step))
+            def _(side=side, step=step):
+                hand_on(side, step).wait()
+
+            @pl.when(sends(side, step))
+            def _(side=side, step=step):
+                hop(side, step, x_ref).wait_send()
 
 
 def gather_pairs(x, axis, collective_id, name):
     n = lax.axis_size(axis)
     vmem = pl.BlockSpec(memory_space=pltpu.VMEM)
-    half = n // 2
+    steps = n // 2 - 1
     dma = pltpu.SemaphoreType.DMA
     return pl.pallas_call(
         functools.partial(gather_pairs_kernel, axis, n),
         out_shape=jax.ShapeDtypeStruct((n * x.shape[0], x.shape[1]), x.dtype),
         in_specs=[vmem],
         out_specs=vmem,
-        scratch_shapes=[dma((half,)), dma((half,)), dma((half,)), dma((half,)), dma(())],
+        scratch_shapes=[dma((2, steps)), dma((2, steps)), dma((2, steps)), dma((2, steps)), dma((3,))],
         compiler_params=pltpu.CompilerParams(
             collective_id=collective_id, has_side_effects=True
         ),
@@ -188,7 +292,17 @@
     tap_total = channelwise_filter_taps.shape[0]
     f32, bf16 = jnp.float32, jnp.bfloat16
 
-    exit_all = lax.all_gather(unitwise_exit_coefficients, "grp", axis=0, tiled=True)
+    half_rows = unitwise_exit_coefficients.shape[0] // 2
+    exit_half = lax.all_gather(
+        lax.dynamic_slice_in_dim(
+            unitwise_exit_coefficients,
+            lax.rem(lax.axis_index("seq"), 2) * half_rows,
+            half_rows,
+            0,
+        ),
+        "grp",
+        axis=0,
+    )
     mixing_all = lax.all_gather(mixing_exit_coefficients, "seq", axis=1, tiled=True)
 
     before = lax.ppermute(
@@ -228,17 +342,30 @@
         ]
     normal_part = layer_norm(mixed_conv, taps_all[tap_total])
     activated = (normal_part * jax.nn.sigmoid(normal_part)).astype(bf16)
+    exit_half, activated = lax.optimization_barrier((exit_half, activated))
+    exit_all = swap_halves(exit_half, "seq", 6, "swap_halves").reshape(
+        feature_width, feature_width
+    )
     residual_part = lax.dynamic_slice_in_dim(acoustic_sequence, grp_index * share, share, 0)
     hidden = (
         residual_part.astype(f32) + jnp.dot(activated, exit_all, preferred_element_type=f32)
     ).astype(bf16)
-    (frames_out,) = exchange(
+    heads = probe_projection_coefficients.shape[1] // head_dim
+    frames_out, queries = exchange(
         [hidden],
         [(frame_count, columns)],
         [(cols_at(columns), rows_at(share))],
         "grp",
         2,
         "to_channels",
+        operands=[
+            textside_token_vectors,
+            textside_rescale_factors[None, :],
+            probe_projection_coefficients,
+            probe_rescale_factors[None, :],
+        ],
+        results=[jax.ShapeDtypeStruct((heads * query_count, head_dim), bf16)],
+        body=query_body,
     )
 
     prior = jnp.cumsum(spike_indicator) - spike_indicator
@@ -292,15 +419,6 @@
         jnp.arange(rows, dtype=jnp.int32)[None, :] < counts.astype(jnp.int32)[:, None]
     ).reshape(blocks * rows)
 
-    dec_normed = rms_scale(
-        textside_token_vectors.astype(f32), textside_rescale_factors
-    ).astype(bf16)
-    query_proj = jnp.dot(
-        dec_normed, probe_projection_coefficients, preferred_element_type=f32
-    ).reshape(query_count, -1, head_dim)
-    queries = rms_scale(query_proj, probe_rescale_factors).astype(bf16)
-    heads = queries.shape[1]
-    queries = queries.transpose(1, 0, 2).reshape(heads * query_count, head_dim)
     scores = (
         lax.dot_general(
             queries, everyone[:, :head_dim], (((1,), (1,)), ((), ())), preferred_element_type=f32

time: 188 us -> 181 us (0.963)
  Pallas kernels: 92.7 us -> 100 us
  matrix products: 24.7 us -> 19.2 us
  other arithmetic: 33.6 us -> 28.5 us
  local copies, waits for them, and re-layouts: 11.5 us -> 9 us
    pallas_call x4 -> x5, Pallas kernels: 75 us -> 80.3 us  [the longest x4 71.7 us: exchange(): pl.pallas_call(functools.partial(exchange_kernel, axis, n, routes, extra)...]
    dot_general x1 -> x0, matrix products: 3.99 us -> none  [local(): jnp.dot(dec_normed, probe_projection_coefficients, preferred_element_type...]
    reduce_sum x3 -> x1, other arithmetic: 3.42 us -> 0.11 us  [rms_scale(): jnp.mean(inputs * inputs, axis=-1, keepdims=True) + EPS_ROOT]
    pallas_call x1, Pallas kernels: 17.6 us -> 20 us  [gather_pairs(): pl.pallas_call(functools.partial(gather_pairs_kernel, axis, n), out_shape...]
    unnamed x43 -> x35, local copies, waits for them, and re-layouts: 5.08 us -> 4.39 us
  transfers between devices with their start and end apart: 5 -> 5, of which waited for: 0 -> 0; matrix products, arithmetic and copies ran while one was open for 31% -> 25% of each run, Pallas kernels for 40% -> 46%
where the time goes in v3:
time: 181 us; the launch traced here: 180 us
  Pallas kernels  100 us (55%)
  other arithmetic  28.5 us (16%)
  matrix products  19.2 us (11%)
  between operations  17 us (9%)
  local copies, waits for them, and re-layouts  9 us (5%)
  starting transfers between devices  5.97 us (3%)
    pallas_call x4, Pallas kernels, exchange(): pl.pallas_call(functools.partial(exchange_kernel, axis, n, routes, extra)...  71.7 us
    pallas_call x1, Pallas kernels, gather_pairs(): pl.pallas_call(functools.partial(gather_pairs_kernel, axis, n), out_shape...  20 us
    reduce_sum x3, other arithmetic, layer_norm(): center = jnp.mean(inputs, axis=-1, keepdims=True)  11.6 us
    pallas_call x1, Pallas kernels, swap_halves(): pl.pallas_call(functools.partial(swap_kernel, axis), out_shape=jax.ShapeD...  8.65 us
    dot_general x1, matrix products, local(): jnp.dot(activated, exit_all, preferred_element_type=f32)  4.87 us
    unnamed x35, local copies, waits for them, and re-layouts  4.39 us
    dot_general x2, matrix products, gate(): projected = jnp.dot(normed, entry, preferred_element_type=f32)  4.19 us
    dot_general x1, matrix products, local(): jnp.dot(attended, mixing_all, preferred_element_type=f32).astype(bf16)  3.92 us
  transfers between devices with their start and end apart: 5, of which 0 were waited for; matrix products, arithmetic and copies ran while one was open for 25% of the time, Pallas kernels for 46%

profile of v3, /device:TPU:0, one launch (start us, length us, event | category | flops | bytes accessed | tf_op | source)
XLA Modules:
  0.0 179.9 jit_solution(14050550885486563362)
XLA Ops:
  7.2 1.2 copy-done
  9.4 1.5 fusion.84
  10.8 3.0 %collective-permute-start = (bf16[16,1536]{1,0:T(8,128)(2,1)}, bf16[16,1536]{1,0:T(8,128)(2,1)}, u32[]{:S(2)}, u32[]{:S(2)}) collective-permute-start(bf16[16,1536]{1,0:T(8,128)(2,1)} %get-tuple-element.49), channel_id=1, source_target_pairs={{0,1},{1,2},{2,3},{3,4},{4,5},{5,6},{6,7},{8,9},{9,10},{10,11},{11... | collective-permute-start | bytes 147464 | tf_op jit(solution)/shard_map/ppermute | solution.py:308
  13.8 1.3 collective-permute-start.1
  15.2 2.5 %convert_reduce_fusion = f32[1024]{0:T(1024)S(1)} fusion(bf16[1024,1536]{1,0:T(8,128)(2,1)} %param.16), kind=kLoop, calls=%fused_computation.1 | loop fusion | flops 3144704 | bytes 3149824 | tf_op jit(solution)/shard_map/reduce_sum | solution.py:257
  18.3 1.6 copy-done.1
  19.8 1.0 fusion.2
  20.8 2.8 %fusion.7 = f32[1024,768]{1,0:T(8,128)S(1)} fusion(bf16[1536,768]{1,0:T(8,128)(2,1)S(1)} %bitcast.41, bf16[1024,1536]{1,0:T(8,128)(2,1)S(1)} %copy-done.1, f32[1536]{0:T(1024)S(1)} %copy-done.11, f32[1024]{0:T(1024)S(1)} %add_rsqrt_fusion, f32[1024]{0:T(1024)S(1)} %broadcast_multiply_fusion), kind=kOutput, calls=%fused_computation.11 | convolution fusion | flops 2423783424 | bytes 8665088 | tf_op jit(solution)/shard_map/dot_general | solution.py:318
  23.6 1.3 fusion.52
  26.0 1.4 fusion.86
  27.4 1.4 pad_maximum_fusion.4.refs_1_
  30.7 1.0 convert_reduce_fusion.3
  31.7 1.0 fusion.67
  32.8 1.4 fusion.70
  34.2 1.0 pad_maximum_fusion.refs_0_
  35.2 26.9 %to_frames.1 = (bf16[288,1536]{1,0:T(8,128)(2,1)}, f32[32,1536]{1,0:T(8,128)}) custom-call(bf16[1056,384]{1,0:T(8,128)(2,1)} %pad_maximum_fusion.refs_0_, f32[32,384]{1,0:T(8,128)} %pad_maximum_fusion.4.refs_1_), custom_call_target="tpu_custom_call" | custom-call | tf_op jit(solution)/shard_map/to_frames/pallas_call | solution.py:111
  62.1 1.4 convert_element_type.91
  64.0 8.1 %fusion.82 = (f32[256]{0:T(256)S(1)}, f32[256,1536]{1,0:T(8,128)S(1)}) fusion(f32[288,1536]{1,0:T(8,128)S(1)} %convert_element_type.91, f32[1536]{0:T(1024)S(1)} %get-tuple-element.16, f32[1536]{0:T(1024)S(1)} %get-tuple-element.17, f32[1536]{0:T(1024)S(1)} %get-tuple-element.18, f32[1536]{0:T(1024)S(1)} %get-tuple-element.19, ...), kind=kLoop, calls=%fused_computation.181 | loop fusion | flops 24379136 | bytes 50523136 | tf_op jit(solution)/shard_map/reduce_sum | solution.py:257
  73.1 8.6 %swap_halves.1 = bf16[4,2,192,1536]{3,2,1,0:T(8,128)(2,1)} custom-call(bf16[4,192,1536]{2,1,0:T(8,128)(2,1)} %bitcast.44), custom_call_target="tpu_custom_call" | custom-call | tf_op jit(solution)/shard_map/swap_halves/pallas_call | solution.py:93
  81.8 4.9 %fusion.12.refs_0_ = bf16[256,1536]{1,0:T(8,128)(2,1)} fusion(bf16[256,1536]{1,0:T(8,128)(2,1)S(1)} %multiply_convert_fusion, bf16[1536,1536]{1,0:T(8,128)(2,1)} %bitcast.43, bf16[1024,1536]{1,0:T(8,128)(2,1)} %param.16, s32[]{:T(128)S(6)} %select_n.24), kind=kOutput, calls=%fused_computation.16 | convolution fusion | flops 1209139200 | bytes 7077892 | tf_op jit(solution)/shard_map/dot_general | solution.py:351
  86.7 15.8 %to_channels.1 = (bf16[1024,384]{1,0:T(8,128)(2,1)}, bf16[512,128]{1,0:T(8,128)(2,1)}) custom-call(bf16[256,1536]{1,0:T(8,128)(2,1)} %fusion.12.refs_0_, bf16[128,4096]{1,0:T(8,128)(2,1)} %refs_1_.1, f32[1,4096]{1,0:T(1,128)} %bitcast.49, bf16[4096,512]{1,0:T(8,128)(2,1)} %refs_3_.1, f32[1,128]{1,0:T(1,128)} %bitcast.51), custom_call_target="tpu_custom_call" | custom-call | tf_op jit(solution)/shard_map/to_channels/pallas_call | solution.py:111
  102.5 2.6 %fusion.49 = f32[256,384]{1,0:T(8,128)S(1)} fusion(bf16[1024,384]{1,0:T(8,128)(2,1)} %get-tuple-element.64, f32[1024]{0:T(1024)S(1)} %copy-done.15, s32[1024]{0:T(1024)S(1)} %get-tuple-element.54), kind=kOutput, calls=%fused_computation.86 | convolution fusion | flops 1209008128 | bytes 1187840 | tf_op jit(solution)/shard_map/dot_general | solution.py:376
  105.1 1.6 collective-permute-start.2
  109.6 11.1 %kv_heads.1 = bf16[4,2,256,128]{3,2,1,0:T(8,128)(2,1)} custom-call(bf16[2,256,512]{2,1,0:T(8,128)(2,1)} %pad_maximum_fusion.1.refs_0_), custom_call_target="tpu_custom_call" | custom-call | tf_op jit(solution)/shard_map/kv_heads/pallas_call | solution.py:111
  120.8 1.2 convert_reduce_fusion.2
  122.9 20.0 %kv_rows.1 = bf16[2176,256]{1,0:T(8,128)(2,1)} custom-call(bf16[272,256]{1,0:T(8,128)(2,1)} %pad_maximum_fusion.2.x_ref), custom_call_target="tpu_custom_call" | custom-call | tf_op jit(solution)/shard_map/kv_rows/pallas_call | solution.py:243
  143.9 2.3 %fusion.87 = (f32[512]{0:T(512)S(1)}, bf16[512,2176]{1,0:T(8,128)(2,1)S(1)}) fusion(bf16[512,128]{1,0:T(8,128)(2,1)S(1)} %copy-done.14, bf16[2176,256]{1,0:T(8,128)(2,1)} %kv_rows.1, pred[2176]{0:T(1024)(128)(4,1)S(1)} %lt.52), kind=kOutput, calls=%fused_computation.185 | convolution fusion | flops 289668608 | bytes 2920576 | tf_op jit(solution)/shard_map/dot_general | solution.py:423
  147.1 3.9 %convolution_convert_fusion.refs_0_ = bf16[128,4096]{1,0:T(8,128)(2,1)} fusion(bf16[128,512]{0,1:T(8,128)(2,1)S(1)} %bitcast.47, bf16[512,4096]{1,0:T(8,128)(2,1)} %all-gather.4.cloned.1.call-done), kind=kOutput, calls=%fused_computation.10 | convolution fusion | flops 537395200 | bytes 5373952 | tf_op jit(solution)/shard_map/dot_general | solution.py:440
  151.0 17.9 %dec_sums.1 = bf16[4,128,1024]{2,1,0:T(8,128)(2,1)} custom-call(bf16[128,4096]{1,0:T(8,128)(2,1)} %convolution_convert_fusion.refs_0_), custom_call_target="tpu_custom_call" | custom-call | tf_op jit(solution)/shard_map/dec_sums/pallas_call | solution.py:111
  169.0 1.5 convert_reduce_fusion.1
  170.5 1.7 add_convert_fusion
  172.2 0.9 copy.25
  (80 shorter events, 9.3 us)
Async XLA Ops:
  7.2 1.3 copy-start
  7.2 65.9 %all-gather.6.cloned.1.call-start = ((), (), s32[]{:S(2)}) async-start(), calls=%async_computation.1 | async-start | bytes 2949120 | tf_op jit(solution)/shard_map/all_gather | solution.py:296
  9.3 137.8 %all-gather.4.cloned.1.call-start = ((), (), s32[]{:S(2)}) async-start(), calls=%async_computation | async-start | bytes 4718592 | tf_op jit(solution)/shard_map/all_gather | solution.py:306
  10.8 19.9 %collective-permute-start = (bf16[16,1536]{1,0:T(8,128)(2,1)}, bf16[16,1536]{1,0:T(8,128)(2,1)}, u32[]{:S(2)}, u32[]{:S(2)}) collective-permute-start(bf16[16,1536]{1,0:T(8,128)(2,1)} %get-tuple-element.49), channel_id=1, source_target_pairs={{0,1},{1,2},{2,3},{3,4},{4,5},{5,6},{6,7},{8,9},{9,10},{10,11},{11... | collective-permute-start | bytes 147464 | tf_op jit(solution)/shard_map/ppermute | solution.py:308
  13.8 16.9 %collective-permute-start.1 = (bf16[16,1536]{1,0:T(8,128)(2,1)}, bf16[16,1536]{1,0:T(8,128)(2,1)}, u32[]{:S(2)}, u32[]{:S(2)}) collective-permute-start(bf16[16,1536]{1,0:T(8,128)(2,1)} %get-tuple-element.50), channel_id=1, source_target_pairs={{1,0},{2,1},{3,2},{4,3},{5,4},{6,5},{7,6},{9,8},{10,9},{11,10},{12... | collective-permute-start | bytes 147464 | tf_op jit(solution)/shard_map/ppermute | solution.py:311
  15.1 2.6 %copy-start.3 = (bf16[1536,2,384]{2,1,0:T(2,128)(2,1)S(1)}, bf16[1536,2,384]{2,1,0:T(2,128)(2,1)}, u32[]{:S(2)}) copy-start(bf16[1536,2,384]{2,1,0:T(2,128)(2,1)} %param.18) | copy-start | bytes 7077892
  17.8 2.1 %copy-start.1 = (bf16[1024,1536]{1,0:T(8,128)(2,1)S(1)}, bf16[1024,1536]{1,0:T(8,128)(2,1)}, u32[]{:S(2)}) copy-start(bf16[1024,1536]{1,0:T(8,128)(2,1)} %param.16) | copy-start | bytes 9437188
  19.8 1.0 copy-start.11
  23.6 1.3 copy-start.12
  23.6 1.9 %copy-start.10 = (s32[1024]{0:T(1024)S(1)}, s32[1024]{0:T(1024)}, u32[]{:S(2)}) copy-start(s32[1024]{0:T(1024)} %param.23) | copy-start | bytes 12292
  30.7 3.5 %copy-start.2 = (bf16[1024,384]{1,0:T(8,128)(2,1)S(1)}, bf16[1024,384]{1,0:T(8,128)(2,1)}, u32[]{:S(2)}) copy-start(bf16[1024,384]{1,0:T(8,128)(2,1)} %fusion.52) | copy-start | bytes 2359300
  62.1 1.4 copy-start.9
  86.7 15.9 %copy-start.15 = (f32[1024]{0:T(1024)S(1)}, f32[1024]{0:T(1024)}, u32[]{:S(2)}) copy-start(f32[1024]{0:T(1024)} %param.22) | copy-start | bytes 12292
  102.5 5.7 %copy-start.7 = (bf16[384,512]{1,0:T(8,128)(2,1)S(1)}, bf16[384,512]{1,0:T(8,128)(2,1)}, u32[]{:S(2)}) copy-start(bf16[384,512]{1,0:T(8,128)(2,1)} %param.28) | copy-start | bytes 1179652
  102.5 6.0 %copy-start.8 = (bf16[384,512]{1,0:T(8,128)(2,1)S(1)}, bf16[384,512]{1,0:T(8,128)(2,1)}, u32[]{:S(2)}) copy-start(bf16[384,512]{1,0:T(8,128)(2,1)} %param.29) | copy-start | bytes 1179652
  105.1 2.9 %collective-permute-start.2 = (f32[1,384]{1,0:T(1,128)S(1)}, f32[1,384]{1,0:T(1,128)S(1)}, u32[]{:S(2)}, u32[]{:S(2)}) collective-permute-start(f32[1,384]{1,0:T(1,128)S(1)} %constant_dynamic-slice_fusion), channel_id=1, source_target_pairs={{0,1},{1,2},{2,3},{3,4},{4,5},{5,6},{6,7},{8,9},{9,10},{10,11},{11... | collective-permute-start | bytes 4616 | tf_op jit(solution)/shard_map/ppermute | solution.py:378
  108.2 12.6 %copy-start.4 = (bf16[256,384]{1,0:T(8,128)(2,1)}, bf16[256,384]{1,0:T(8,128)(2,1)S(1)}, u32[]{:S(2)}) copy-start(bf16[256,384]{1,0:T(8,128)(2,1)S(1)} %select_convert_fusion) | copy-start | bytes 589828
  108.8 13.3 %copy-start.13 = (f32[128]{0:T(128)S(1)}, f32[128]{0:T(128)}, u32[]{:S(2)}) copy-start(f32[128]{0:T(128)} %param.30) | copy-start | bytes 1540
  120.8 23.1 %copy-start.14 = (bf16[512,128]{1,0:T(8,128)(2,1)S(1)}, bf16[512,128]{1,0:T(8,128)(2,1)}, u32[]{:S(2)}) copy-start(bf16[512,128]{1,0:T(8,128)(2,1)} %get-tuple-element.14) | copy-start | bytes 393220
  143.9 2.3 %copy-start.5 = (bf16[2176,256]{1,0:T(8,128)(2,1)S(1)}, bf16[2176,256]{1,0:T(8,128)(2,1)}, u32[]{:S(2)}) copy-start(bf16[2176,256]{1,0:T(8,128)(2,1)} %kv_rows.1) | copy-start | bytes 3342340
  168.9 3.3 %copy-start.6 = (bf16[1024,384]{1,0:T(8,128)(2,1)S(1)}, bf16[1024,384]{1,0:T(8,128)(2,1)}, u32[]{:S(2)}) copy-start(bf16[1024,384]{1,0:T(8,128)(2,1)} %get-tuple-element.64) | copy-start | bytes 2359300
Sparse Core Ops, SparseCore 0:
  9.8 51.4 all-gather.5
  62.9 47.1 all-gather.3

commit v4 on v2

--- a/solution.py
+++ b/solution.py
@@ -85,6 +85,65 @@
         ),
         name=name,
     )(*arrays)
+
+
+def product_kernel(axis, n, a_ref, w_ref, r_ref, o_ref, out_buf, parts, send, recv):
+    width = parts.shape[2]
+    me = lax.axis_index(axis)
+    barrier = pltpu.get_barrier_semaphore()
+    for k in range(1, n):
+        pl.semaphore_signal(
+            barrier, inc=1, device_id={axis: lax.rem(me + k, n)}, device_id_type=MESH
+        )
+
+    def product(i):
+        columns = pl.ds(pl.multiple_of(i * width, width), width)
+        return jnp.dot(a_ref[...], w_ref[:, columns], preferred_element_type=jnp.float32)
+
+    copies = []
+    for k in range(1, n):
+        peer = lax.rem(me + k, n)
+        out_buf[k - 1] = product(peer).astype(out_buf.dtype)
+        if k == 1:
+            pl.semaphore_wait(barrier, n - 1)
+        copy = pltpu.make_async_remote_copy(
+            src_ref=out_buf.at[k - 1],
+            dst_ref=parts.at[k - 1],
+            send_sem=send.at[k - 1],
+            recv_sem=recv.at[k - 1],
+            device_id={axis: peer},
+            device_id_type=MESH,
+        )
+        copy.start()
+        copies.append(copy)
+    total = r_ref[...].astype(jnp.float32) + product(me)
+    for k in range(1, n):
+        copies[k - 1].wait()
+        total = total + parts[k - 1].astype(jnp.float32)
+    o_ref[...] = total.astype(o_ref.dtype)
+
+
+def product_sum(a, w, r, axis, collective_id, name):
+    n = lax.axis_size(axis)
+    vmem = pl.BlockSpec(memory_space=pltpu.VMEM)
+    dma = pltpu.SemaphoreType.DMA
+    shape = (n - 1,) + r.shape
+    return pl.pallas_call(
+        functools.partial(product_kernel, axis, n),
+        out_shape=jax.ShapeDtypeStruct(r.shape, r.dtype),
+        in_specs=[vmem] * 3,
+        out_specs=vmem,
+        scratch_shapes=[
+            pltpu.VMEM(shape, jnp.bfloat16),
+            pltpu.VMEM(shape, jnp.bfloat16),
+            dma((n - 1,)),
+            dma((n - 1,)),
+        ],
+        compiler_params=pltpu.CompilerParams(
+            collective_id=collective_id, has_side_effects=True
+        ),
+        name=name,
+    )(a, w, r)
 
 
 def rows_at(size, length=None):
@@ -354,20 +413,11 @@
         .transpose(1, 0, 2)
         .reshape(query_count, heads * head_dim)
     )
-    partial_out = jnp.dot(attended, mixing_all, preferred_element_type=f32).astype(bf16)
     out_width = text_width // groups
-    (parts,) = exchange(
-        [partial_out],
-        [(groups, query_count, out_width)],
-        [(cols_at(out_width), slab)],
-        "grp",
-        5,
-        "dec_sums",
-    )
     residual_dec = lax.dynamic_slice_in_dim(
         textside_token_vectors, grp_index * out_width, out_width, 1
-    ).astype(f32)
-    dec_out = (residual_dec + jnp.sum(parts.astype(f32), axis=0)).astype(bf16)
+    )
+    dec_out = product_sum(attended, mixing_all, residual_dec, "grp", 5, "dec_sums")
     return (frames_out, pooled_local, dec_out)
 
 

time: 175 us -> 172 us (0.983)
  matrix products: 21.9 us -> 17.9 us
  other arithmetic: 33.5 us -> 30.3 us
  local copies, waits for them, and re-layouts: 11.7 us -> 14.8 us
  Pallas kernels: 81.2 us -> 83.3 us
  waiting for transfers between devices: 2.55 us -> 0.75 us
    pallas_call x0 -> x1, Pallas kernels: none -> 18.9 us  [product_sum(): pl.pallas_call(functools.partial(product_kernel, axis, n), out_shape=jax....]
    pallas_call x4 -> x3, Pallas kernels: 64.3 us -> 47.5 us  [exchange(): pl.pallas_call(functools.partial(exchange_kernel, axis, n, routes, swap),...]
    dot_general x1 -> x0, matrix products: 3.93 us -> none  [local(): jnp.dot(attended, mixing_all, preferred_element_type=f32).astype(bf16)]
    all_gather x1, waiting for transfers between devices: 2.49 us -> 0.71 us  [local(): lax.all_gather(lax.dynamic_slice_in_dim(unitwise_exit_coefficients, lax.r...]
    unnamed x45 -> x47, local copies, waits for them, and re-layouts: 4.41 us -> 5.96 us
  transfers between devices with their start and end apart: 5 -> 5, of which waited for: 1 -> 1; matrix products, arithmetic and copies ran while one was open for 32% -> 34% of each run, Pallas kernels for 36% -> 38%
where the time goes in v4:
time: 172 us; the launch traced here: 171 us
  Pallas kernels  83.3 us (48%)
  other arithmetic  30.3 us (18%)
  matrix products  17.9 us (10%)
  between operations  17.1 us (10%)
  local copies, waits for them, and re-layouts  14.8 us (9%)
  starting transfers between devices  6.36 us (4%)
    pallas_call x3, Pallas kernels, exchange(): pl.pallas_call(functools.partial(exchange_kernel, axis, n, routes, swap),...  47.5 us
    pallas_call x1, Pallas kernels, product_sum(): pl.pallas_call(functools.partial(product_kernel, axis, n), out_shape=jax....  18.9 us
    pallas_call x1, Pallas kernels, gather_pairs(): pl.pallas_call(functools.partial(gather_pairs_kernel, axis, n), out_shape...  16.9 us
    reduce_sum x3, other arithmetic, layer_norm(): center = jnp.mean(inputs, axis=-1, keepdims=True)  11.6 us
    unnamed x47, local copies, waits for them, and re-layouts  5.96 us
    dot_general x2, matrix products, gate(): projected = jnp.dot(normed, entry, preferred_element_type=f32)  4.17 us
    dot_general x1, matrix products, local(): jnp.dot(dec_normed, probe_projection_coefficients, preferred_element_type...  4 us
    dot_general x1, matrix products, local(): jnp.dot(activated, exit_all, preferred_element_type=f32)  3.64 us
  transfers between devices with their start and end apart: 5, of which 1 were waited for; matrix products, arithmetic and copies ran while one was open for 34% of the time, Pallas kernels for 38%

profile of v4, /device:TPU:0, one launch (start us, length us, event | category | flops | bytes accessed | tf_op | source)
XLA Modules:
  0.0 170.6 jit_solution(714379949869519360)
XLA Ops:
  7.2 1.2 copy-done
  9.4 1.5 fusion.98
  10.8 3.0 %collective-permute-start = (bf16[16,1536]{1,0:T(8,128)(2,1)}, bf16[16,1536]{1,0:T(8,128)(2,1)}, u32[]{:S(2)}, u32[]{:S(2)}) collective-permute-start(bf16[16,1536]{1,0:T(8,128)(2,1)} %get-tuple-element.43), channel_id=1, source_target_pairs={{0,1},{1,2},{2,3},{3,4},{4,5},{5,6},{6,7},{8,9},{9,10},{10,11},{11... | collective-permute-start | bytes 147464 | tf_op jit(solution)/shard_map/ppermute | solution.py:282
  13.8 1.3 collective-permute-start.1
  15.2 2.5 %convert_reduce_fusion = f32[1024]{0:T(1024)S(1)} fusion(bf16[1024,1536]{1,0:T(8,128)(2,1)} %param.16), kind=kLoop, calls=%fused_computation.1 | loop fusion | flops 3144704 | bytes 3149824 | tf_op jit(solution)/shard_map/reduce_sum | solution.py:231
  18.3 1.6 copy-done.1
  20.8 2.8 %fusion.7 = f32[1024,768]{1,0:T(8,128)S(1)} fusion(bf16[1536,768]{1,0:T(8,128)(2,1)S(1)} %bitcast.51, bf16[1024,1536]{1,0:T(8,128)(2,1)S(1)} %copy-done.1, f32[1536]{0:T(1024)S(1)} %copy-done.13, f32[1024]{0:T(1024)S(1)} %add_rsqrt_fusion, f32[1024]{0:T(1024)S(1)} %broadcast_multiply_fusion), kind=kOutput, calls=%fused_computation.10 | convolution fusion | flops 2423783424 | bytes 8665088 | tf_op jit(solution)/shard_map/dot_general | solution.py:292
  23.6 1.3 fusion.55
  26.0 2.0 %fusion.100 = (s32[]{:T(128)}, s32[1024]{0:T(1024)}) fusion(s32[1024]{0:T(1024)} %param.23, s32[8,128]{1,0:T(8,128)S(1)} %reduce-window.9, s32[8]{0:T(128)S(1)} %slice_reduce_fusion.32), kind=kLoop, calls=%fused_computation.202 | loop fusion | flops 3071 | bytes 12324 | tf_op jit(solution)/shard_map/reduce_sum | solution.py:339
  28.0 1.5 fusion.15
  29.5 4.0 %fusion.64 = f32[128,512]{1,0:T(8,128)} fusion(bf16[4096,512]{1,0:T(8,128)(2,1)} %param.26, bf16[128,4096]{1,0:T(8,128)(2,1)} %param.24, f32[4096]{0:T(1024)} %param.25, f32[128]{0:T(128)S(1)} %add_rsqrt_fusion.4), kind=kOutput, calls=%fused_computation.101 | convolution fusion | flops 538968064 | bytes 5521920 | tf_op jit(solution)/shard_map/dot_general | solution.py:392
  33.5 1.7 %reshape.145 = f32[128,4,128]{2,1,0:T(4,128)} reshape(f32[128,512]{1,0:T(8,128)} %fusion.64) | data formatting | bytes 524288 | tf_op jit(solution)/shard_map/reshape | solution.py:394
  35.2 1.8 %multiply_reduce_fusion.1 = f32[128,4]{1,0:T(8,128)} fusion(f32[128,4,128]{2,1,0:T(4,128)} %reshape.145), kind=kLoop, calls=%fused_computation.120 | loop fusion | flops 130560 | bytes 264192 | tf_op jit(solution)/shard_map/reduce_sum | solution.py:237
  37.9 1.7 %constant_dynamic-slice_fusion.r_ref = bf16[128,1024]{1,0:T(8,128)(2,1)} fusion(bf16[128,4096]{1,0:T(8,128)(2,1)} %param.24, s32[]{:T(128)S(6)} %select_n.30), kind=kLoop, calls=%fused_computation.189 | loop fusion | bytes 524292 | tf_op jit(solution)/shard_map/dynamic_slice | solution.py:417
  39.7 1.8 %fusion.77 = bf16[128,4,128]{2,0,1:T(8,128)(2,1)} fusion(f32[128]{0:T(128)} %param.27, f32[128,4]{0,1:T(4,128)S(1)} %add_rsqrt_fusion.1, f32[128,512]{1,0:T(8,128)} %fusion.64), kind=kLoop, calls=%fused_computation.119 | loop fusion | flops 196608 | bytes 395776 | tf_op jit(solution)/shard_map/convert_element_type | solution.py:395
  41.4 1.4 pad_maximum_fusion.4.refs_1_
  44.8 1.0 convert_reduce_fusion.2
  45.8 1.0 fusion.80
  46.8 1.4 fusion.83
  48.3 1.0 pad_maximum_fusion.refs_0_
  50.0 21.7 %to_frames.1 = (bf16[288,1536]{1,0:T(8,128)(2,1)}, f32[32,1536]{1,0:T(8,128)}, bf16[4,2,192,1536]{3,2,1,0:T(8,128)(2,1)}) custom-call(bf16[1056,384]{1,0:T(8,128)(2,1)} %pad_maximum_fusion.refs_0_, f32[32,384]{1,0:T(8,128)} %pad_maximum_fusion.4.refs_1_, bf16[4,192,1536]{2,1,0:T(8,128)(2,1)} %bitcast.54), custom_call_target="tpu_custom_call" | custom-call | tf_op jit(solution)/shard_map/to_frames/pallas_call | solution.py:73
  71.7 1.4 convert_element_type.88
  73.7 8.1 %fusion.96 = (f32[256]{0:T(256)S(1)}, f32[256,1536]{1,0:T(8,128)S(1)}) fusion(f32[288,1536]{1,0:T(8,128)S(1)} %convert_element_type.88, f32[1536]{0:T(1024)S(1)} %get-tuple-element.10, f32[1536]{0:T(1024)S(1)} %get-tuple-element.11, f32[1536]{0:T(1024)S(1)} %get-tuple-element.12, f32[1536]{0:T(1024)S(1)} %get-tuple-element.13, ...), kind=kLoop, calls=%fused_computation.199 | loop fusion | flops 24379136 | bytes 50523136 | tf_op jit(solution)/shard_map/reduce_sum | solution.py:231
  82.1 3.6 %fusion.12.refs_0_ = bf16[256,1536]{1,0:T(8,128)(2,1)} fusion(bf16[1536,1536]{1,0:T(8,128)(2,1)S(1)} %bitcast.63, f32[256,1536]{1,0:T(8,128)S(1)} %get-tuple-element.42, f32[1536]{0:T(1024)S(1)} %get-tuple-element.9, f32[256]{0:T(256)S(1)} %add_rsqrt_fusion.3, f32[256]{0:T(256)S(1)} %broadcast_multiply_fusion.1, bf16[1024,1536]{1,0:T(8,128)(2,1)} %param.16, ...), kind=kOutput, calls=%fused_computation.17 | convolution fusion | flops 1212284928 | bytes 7872516 | tf_op jit(solution)/shard_map/dot_general | solution.py:327
  85.7 14.4 %to_channels.1 = bf16[1024,384]{1,0:T(8,128)(2,1)} custom-call(bf16[256,1536]{1,0:T(8,128)(2,1)} %fusion.12.refs_0_), custom_call_target="tpu_custom_call" | custom-call | tf_op jit(solution)/shard_map/to_channels/pallas_call | solution.py:73
  100.2 2.5 %fusion.52 = f32[256,384]{1,0:T(8,128)S(1)} fusion(bf16[1024,384]{1,0:T(8,128)(2,1)} %to_channels.1, f32[1024]{0:T(1024)S(1)} %copy-done.18, s32[1024]{0:T(1024)S(1)} %copy-done.15), kind=kOutput, calls=%fused_computation.89 | convolution fusion | flops 1209008128 | bytes 1187840 | tf_op jit(solution)/shard_map/dot_general | solution.py:343
  102.8 2.0 %collective-permute-start.2 = (f32[1,384]{1,0:T(1,128)S(1)}, f32[1,384]{1,0:T(1,128)S(1)}, u32[]{:S(2)}, u32[]{:S(2)}) collective-permute-start(f32[1,384]{1,0:T(1,128)S(1)} %constant_dynamic-slice_fusion.1), channel_id=1, source_target_pairs={{0,1},{1,2},{2,3},{3,4},{4,5},{5,6},{6,7},{8,9},{9,10},{10,11},{11... | collective-permute-start | bytes 4616 | tf_op jit(solution)/shard_map/ppermute | solution.py:345
  107.7 11.4 %kv_heads.1 = bf16[4,2,256,128]{3,2,1,0:T(8,128)(2,1)} custom-call(bf16[2,256,512]{2,1,0:T(8,128)(2,1)} %pad_maximum_fusion.1.refs_0_), custom_call_target="tpu_custom_call" | custom-call | tf_op jit(solution)/shard_map/kv_heads/pallas_call | solution.py:73
  119.2 1.2 convert_reduce_fusion.1
  121.3 16.9 %kv_rows.1 = bf16[2176,256]{1,0:T(8,128)(2,1)} custom-call(bf16[272,256]{1,0:T(8,128)(2,1)} %pad_maximum_fusion.2.x_ref), custom_call_target="tpu_custom_call" | custom-call | tf_op jit(solution)/shard_map/kv_rows/pallas_call | solution.py:217
  139.2 2.3 %fusion.101 = (f32[512]{0:T(512)S(1)}, bf16[512,2176]{1,0:T(8,128)(2,1)S(1)}) fusion(bf16[512,128]{1,0:T(8,128)(2,1)S(1)} %bitcast.58, bf16[2176,256]{1,0:T(8,128)(2,1)} %kv_rows.1, pred[2176]{0:T(1024)(128)(4,1)S(1)} %lt.51), kind=kOutput, calls=%fused_computation.203 | convolution fusion | flops 289668608 | bytes 2920576 | tf_op jit(solution)/shard_map/dot_general | solution.py:399
  143.1 18.9 %dec_sums.1 = bf16[128,1024]{1,0:T(8,128)(2,1)} custom-call(bf16[128,512]{1,0:T(8,128)(2,1)} %bitcast.56, bf16[512,4096]{1,0:T(8,128)(2,1)} %all-gather.4.cloned.1.call-done.w_ref, bf16[128,1024]{1,0:T(8,128)(2,1)} %constant_dynamic-slice_fusion.r_ref), custom_call_target="tpu_custom_call" | custom-call | tf_op jit(solution)/shard_map/dec_sums/pallas_call | solution.py:131
  (97 shorter events, 13.6 us)
Async XLA Ops:
  7.2 1.3 copy-start
  7.2 42.8 %all-gather.6.cloned.1.call-start = ((), (), s32[]{:S(2)}) async-start(), calls=%async_computation.1 | async-start | bytes 2949120 | tf_op jit(solution)/shard_map/all_gather | solution.py:270
  9.3 133.7 %all-gather.4.cloned.1.call-start = ((), (), s32[]{:S(2)}) async-start(), calls=%async_computation | async-start | bytes 4718592 | tf_op jit(solution)/shard_map/all_gather | solution.py:280
  10.8 33.9 %collective-permute-start = (bf16[16,1536]{1,0:T(8,128)(2,1)}, bf16[16,1536]{1,0:T(8,128)(2,1)}, u32[]{:S(2)}, u32[]{:S(2)}) collective-permute-start(bf16[16,1536]{1,0:T(8,128)(2,1)} %get-tuple-element.43), channel_id=1, source_target_pairs={{0,1},{1,2},{2,3},{3,4},{4,5},{5,6},{6,7},{8,9},{9,10},{10,11},{11... | collective-permute-start | bytes 147464 | tf_op jit(solution)/shard_map/ppermute | solution.py:282
  13.8 30.9 %collective-permute-start.1 = (bf16[16,1536]{1,0:T(8,128)(2,1)}, bf16[16,1536]{1,0:T(8,128)(2,1)}, u32[]{:S(2)}, u32[]{:S(2)}) collective-permute-start(bf16[16,1536]{1,0:T(8,128)(2,1)} %get-tuple-element.44), channel_id=1, source_target_pairs={{1,0},{2,1},{3,2},{4,3},{5,4},{6,5},{7,6},{9,8},{10,9},{11,10},{12... | collective-permute-start | bytes 147464 | tf_op jit(solution)/shard_map/ppermute | solution.py:285
  15.2 2.6 %copy-start.4 = (bf16[1536,2,384]{2,1,0:T(2,128)(2,1)S(1)}, bf16[1536,2,384]{2,1,0:T(2,128)(2,1)}, u32[]{:S(2)}) copy-start(bf16[1536,2,384]{2,1,0:T(2,128)(2,1)} %param.18) | copy-start | bytes 7077892
  17.8 2.1 %copy-start.1 = (bf16[1024,1536]{1,0:T(8,128)(2,1)S(1)}, bf16[1024,1536]{1,0:T(8,128)(2,1)}, u32[]{:S(2)}) copy-start(bf16[1024,1536]{1,0:T(8,128)(2,1)} %param.16) | copy-start | bytes 9437188
  19.8 1.0 copy-start.13
  23.6 1.3 copy-start.16
  23.6 1.9 %copy-start.12 = (s32[1024]{0:T(1024)S(1)}, s32[1024]{0:T(1024)}, u32[]{:S(2)}) copy-start(s32[1024]{0:T(1024)} %param.23) | copy-start | bytes 12292
  33.5 13.3 %copy-start.14 = (f32[1536]{0:T(1024)S(1)}, f32[1536]{0:T(1024)}, u32[]{:S(2)}) copy-start(f32[1536]{0:T(1024)} %param.17) | copy-start | bytes 18436
  44.7 3.5 %copy-start.3 = (bf16[1024,384]{1,0:T(8,128)(2,1)S(1)}, bf16[1024,384]{1,0:T(8,128)(2,1)}, u32[]{:S(2)}) copy-start(bf16[1024,384]{1,0:T(8,128)(2,1)} %fusion.55) | copy-start | bytes 2359300
  71.7 1.4 copy-start.10
  73.6 8.4 %slice-start = ((s8[4718592]{0:T(1024)(128)(4,1)}), s8[4194304]{0:T(1024)(128)(4,1)S(1)}, s32[]{:S(2)}) async-start(s8[4718592]{0:T(1024)(128)(4,1)} %bitcast.61), calls=%async_computation.2 | async-start | bytes 8388608
  73.6 8.4 %slice-start.1 = ((s8[4718592]{0:T(1024)(128)(4,1)}), s8[524288]{0:T(1024)(128)(4,1)S(1)}, s32[]{:S(2)}) async-start(s8[4718592]{0:T(1024)(128)(4,1)} %bitcast.61), calls=%async_computation.3 | async-start | bytes 1048576
  85.7 14.5 %copy-start.15 = (s32[1024]{0:T(1024)S(1)}, s32[1024]{0:T(1024)}, u32[]{:S(2)}) copy-start(s32[1024]{0:T(1024)} %get-tuple-element.48) | copy-start | bytes 12292
  85.7 14.5 %copy-start.18 = (f32[1024]{0:T(1024)S(1)}, f32[1024]{0:T(1024)}, u32[]{:S(2)}) copy-start(f32[1024]{0:T(1024)} %param.22) | copy-start | bytes 12292
  85.7 20.5 %copy-start.8 = (bf16[384,512]{1,0:T(8,128)(2,1)S(1)}, bf16[384,512]{1,0:T(8,128)(2,1)}, u32[]{:S(2)}) copy-start(bf16[384,512]{1,0:T(8,128)(2,1)} %param.28) | copy-start | bytes 1179652
  100.2 6.4 %copy-start.9 = (bf16[384,512]{1,0:T(8,128)(2,1)S(1)}, bf16[384,512]{1,0:T(8,128)(2,1)}, u32[]{:S(2)}) copy-start(bf16[384,512]{1,0:T(8,128)(2,1)} %param.29) | copy-start | bytes 1179652
  102.8 3.3 %collective-permute-start.2 = (f32[1,384]{1,0:T(1,128)S(1)}, f32[1,384]{1,0:T(1,128)S(1)}, u32[]{:S(2)}, u32[]{:S(2)}) collective-permute-start(f32[1,384]{1,0:T(1,128)S(1)} %constant_dynamic-slice_fusion.1), channel_id=1, source_target_pairs={{0,1},{1,2},{2,3},{3,4},{4,5},{5,6},{6,7},{8,9},{9,10},{10,11},{11... | collective-permute-start | bytes 4616 | tf_op jit(solution)/shard_map/ppermute | solution.py:345
  106.3 12.9 %copy-start.5 = (bf16[256,384]{1,0:T(8,128)(2,1)}, bf16[256,384]{1,0:T(8,128)(2,1)S(1)}, u32[]{:S(2)}) copy-start(bf16[256,384]{1,0:T(8,128)(2,1)S(1)} %select_convert_fusion) | copy-start | bytes 589828
  106.9 13.6 %copy-start.17 = (f32[128]{0:T(128)S(1)}, f32[128]{0:T(128)}, u32[]{:S(2)}) copy-start(f32[128]{0:T(128)} %param.30) | copy-start | bytes 1540
  119.2 20.0 %copy-start.11 = (bf16[128,4,128]{2,0,1:T(8,128)(2,1)S(1)}, bf16[128,4,128]{2,0,1:T(8,128)(2,1)}, u32[]{:S(2)}) copy-start(bf16[128,4,128]{2,0,1:T(8,128)(2,1)} %fusion.77) | copy-start | bytes 393220
  139.2 2.3 %copy-start.6 = (bf16[2176,256]{1,0:T(8,128)(2,1)S(1)}, bf16[2176,256]{1,0:T(8,128)(2,1)}, u32[]{:S(2)}) copy-start(bf16[2176,256]{1,0:T(8,128)(2,1)} %kv_rows.1) | copy-start | bytes 3342340
  143.1 18.9 %copy-start.2 = (bf16[1024,384]{1,0:T(8,128)(2,1)S(1)}, bf16[1024,384]{1,0:T(8,128)(2,1)}, u32[]{:S(2)}) copy-start(bf16[1024,384]{1,0:T(8,128)(2,1)} %to_channels.1) | copy-start | bytes 2359300
  162.0 1.1 copy-start.7
Sparse Core Ops, SparseCore 0:
  9.8 40.1 all-gather.5
  51.6 46.8 all-gather.3
